TPU v7x, 512 devices: a whole 4x4x16 slice. The times are simulated.
512 devices in a mesh: dp: 32 (over x, y, core), fsdp: 16 (over z).
Axes of the slice: x: 4, y: 4, z: 16, core: 2. Of those that a mesh axis runs over, the one named last changes fastest.
Arguments:
- query_pooled_states: bfloat16 [16, 512, 4096], P('fsdp', 'dp')
- passage_pooled_states: bfloat16 [16, 4096, 4096], P('fsdp', 'dp')
- query_attention_output: bfloat16 [16, 512, 4096], P('fsdp', 'dp'), may hold values from -0.059814453 to 0.059814453
- passage_attention_output: bfloat16 [16, 4096, 4096], P('fsdp', 'dp'), may hold values from -0.059814453 to 0.059814453
- positive_passage_row: int32 [16, 512], P('fsdp', 'dp'), may hold values from 0 to 127
- hard_negative_ids: int32 [16, 512, 64], P('fsdp', 'dp'), may hold values from 0 to 4095, as said below
- passage_home_row: int32 [16, 4096], P('fsdp'), may hold values from 0 to 4095, as said below
- adapter_down_weight: bfloat16 [16, 4096], P(None, 'fsdp'), may hold values from -0.09375 to 0.09375
- adapter_up_weight: bfloat16 [16, 4096], P(None, 'fsdp'), may hold values from -0.09375 to 0.09375
Outputs:
- grad_query_states: bfloat16 [16, 512, 4096], P('fsdp', 'dp')
- grad_passage_states: bfloat16 [16, 4096, 4096], P('fsdp', 'dp')
- adapter_down_gradient: float32 [16, 4096], P(None, 'fsdp')
- adapter_up_gradient: float32 [16, 4096], P(None, 'fsdp')
Inputs may be any that keep to these rules, and one draw needn't show every extreme that they name: In each group the row is a permutation: passage p is row passage_home_row[g, p] of passage_pooled_states[g]. `hard_negative_ids`: ids of passages of the same group. The queries of one index of dp name at most 8 distinct passages held by any one index of dp, and in every group one index of dp holds exactly 8 distinct passages named by the queries of each index of dp. A query's list may repeat an id. `positive_passage_row`: the positive of query q is held by the query's own index of dp.
All inputs are finite; a program needn't handle non-finite values.
Results may differ from a plain program's by a relative error of at most 0.0062.
Values may be sent and summed in bfloat16 or wider, within the bound.
A program may use at most 64 MiB of HBM per device.

v0:
```python
import jax
import jax.numpy as jnp
from jax import lax
from jax.sharding import PartitionSpec as P

NEG = 64
CAP = 8
P_DEV = 128


SOFTMAX_HEAT = 0.01
ADAPTER_SCALE = 2.0
EPSILON = 1e-06


def sent_together(arrays, axis, dim, along):
    both = jnp.concatenate(arrays, axis=along)
    whole, at, gathered = (lax.all_gather(both, axis, axis=dim, tiled=True), 0, [])
    for a in arrays:
        gathered.append(lax.slice_in_dim(whole, at, at + a.shape[along], axis=along))
        at += a.shape[along]
    return tuple(gathered)


def in_blocks(array, dim, peers):
    before, after = (array.shape[:dim], array.shape[dim + 1 :])
    return jnp.moveaxis(array.reshape(*before, peers, -1, *after), dim, 0)


def sum_at_owner(array, axis, dim):
    tiles = in_blocks(array, dim, lax.axis_size(axis))
    arrived = lax.all_to_all(tiles, axis, split_axis=0, concat_axis=0, tiled=True)
    return arrived.sum(axis=0)


def in_one_piece(arrays, axis, dim, along):
    widths = [a.shape[along] for a in arrays]
    both = jnp.concatenate(arrays, axis=along)
    whole = sum_at_owner(both, axis, dim)
    return tuple(jnp.split(whole, [sum(widths[:k]) for k in range(1, len(widths))], axis=along))


def sent_to_all(array, axis):
    peers = lax.axis_size(axis)
    return lax.all_to_all(
        jnp.broadcast_to(array[None], (peers, *array.shape)), axis, 0, 0, tiled=True
    )


def over_copies(array, axis):
    everything = sent_to_all(array, axis)
    return jnp.sum(everything, axis=0)


def together(arrays, axis):
    ends = [0]
    for a in arrays:
        ends.append(ends[-1] + a.size)
    running = over_copies(jnp.concatenate([a.ravel() for a in arrays]), axis)
    return tuple((running[b:e].reshape(a.shape) for a, b, e in zip(arrays, ends, ends[1:])))


def unit_rows(raw_rows):
    values = raw_rows.astype(jnp.float32)
    lengths = jnp.sqrt(jnp.sum(values * values, axis=-1, keepdims=True) + EPSILON)
    return (values / lengths, lengths)


def norm_backward(unit_vec, lengths, upstream):
    inner_sum = jnp.sum(unit_vec * upstream, axis=-1, keepdims=True)
    return ((upstream - unit_vec * inner_sum) / lengths).astype(jnp.bfloat16)


def per_device(
    query_pooled_states,
    passage_pooled_states,
    query_attention_output,
    passage_attention_output,
    positive_passage_row,
    hard_negative_ids,
    passage_home_row,
    adapter_down_weight,
    adapter_up_weight,
):
    query_unit, query_length = unit_rows(query_pooled_states[0])
    passage_unit, passage_length = unit_rows(passage_pooled_states[0])
    query_vectors = query_unit.astype(jnp.bfloat16)
    passage_vectors = passage_unit.astype(jnp.bfloat16)
    group_size = lax.axis_size("dp")
    slot_count = group_size * CAP
    home_rows = passage_home_row[0]
    negative_rows = home_rows[hard_negative_ids[0]]
    owners = negative_rows // P_DEV
    marked = jnp.zeros((group_size * P_DEV,), jnp.int32).at[negative_rows.reshape(-1)].max(1)
    marked_grid = marked.reshape(group_size, P_DEV)
    rank_grid = jnp.cumsum(marked_grid, axis=1) - 1
    owner_grid = jnp.broadcast_to(
        jnp.arange(group_size, dtype=jnp.int32)[:, None], (group_size, P_DEV)
    )
    row_grid = jnp.broadcast_to(jnp.arange(P_DEV, dtype=jnp.int32)[None, :], (group_size, P_DEV))
    column_grid = jnp.where(marked_grid > 0, rank_grid, CAP)
    requests = (
        jnp.zeros((group_size, CAP), jnp.int32)
        .at[owner_grid, column_grid]
        .set(row_grid, mode="drop")
    )
    request_slot = owners * CAP + rank_grid.reshape(-1)[negative_rows]
    requested = lax.all_to_all(requests, "dp", split_axis=0, concat_axis=0, tiled=True)
    rows_out = passage_vectors[requested]
    fetched = lax.all_to_all(rows_out, "dp", split_axis=0, concat_axis=0, tiled=True)
    gathered_flat_rows = fetched.reshape(slot_count, fetched.shape[-1])
    slot_scores = (
        jnp.dot(query_vectors, gathered_flat_rows.T, preferred_element_type=jnp.float32)
        / SOFTMAX_HEAT
    )
    negative_scores = jnp.take_along_axis(slot_scores, request_slot, axis=1)
    positives = positive_passage_row[0]
    positive_embed = passage_vectors[positives]
    positive_scores = (
        jnp.sum(query_vectors.astype(jnp.float32) * positive_embed.astype(jnp.float32), axis=-1)
        / SOFTMAX_HEAT
    )
    scores = jnp.concatenate([positive_scores[:, None], negative_scores], axis=1)
    row_max = jnp.max(scores, axis=-1, keepdims=True)
    raised = jnp.exp(scores - row_max)
    softmax_probabilities = raised / jnp.sum(raised, axis=-1, keepdims=True)
    target_index = (jnp.arange(NEG + 1) == 0).astype(jnp.float32)
    score_gradient = (softmax_probabilities - target_index[None, :]) / SOFTMAX_HEAT
    positive_weight = score_gradient[:, 0]
    negative_weight = score_gradient[:, 1:]
    slot_match = (
        request_slot[:, :, None] == jnp.arange(slot_count, dtype=jnp.int32)[None, None, :]
    ).astype(jnp.float32)
    slot_weight = jnp.einsum(
        "qjs,qj->qs", slot_match, negative_weight, precision=lax.Precision.HIGHEST
    )
    query_upstream = jnp.dot(
        slot_weight, gathered_flat_rows.astype(jnp.float32), precision=lax.Precision.HIGHEST
    )
    query_upstream = query_upstream + positive_weight[:, None] * positive_embed.astype(jnp.float32)
    query_gradient = norm_backward(query_unit, query_length, query_upstream)
    query_float = query_vectors.astype(jnp.float32)
    positive_match = (positives[None, :] == jnp.arange(P_DEV, dtype=jnp.int32)[:, None]).astype(
        jnp.float32
    )
    passage_upstream = jnp.dot(
        positive_match * positive_weight[None, :], query_float, precision=lax.Precision.HIGHEST
    )
    gathered_queries = lax.all_gather(query_vectors, "dp", axis=0, tiled=True)
    sent_weight = lax.all_to_all(
        slot_weight.T.reshape(group_size, CAP, slot_weight.shape[0]),
        "dp",
        split_axis=0,
        concat_axis=0,
        tiled=True,
    )
    served_onehot = (
        requested[:, :, None] == jnp.arange(P_DEV, dtype=jnp.int32)[None, None, :]
    ).astype(jnp.float32)
    owner_weight = jnp.einsum(
        "rcp,rcq->prq", served_onehot, sent_weight, precision=lax.Precision.HIGHEST
    ).reshape(P_DEV, gathered_queries.shape[0])
    passage_upstream = passage_upstream + jnp.dot(
        owner_weight, gathered_queries.astype(jnp.float32), precision=lax.Precision.HIGHEST
    )
    passage_gradient = norm_backward(passage_unit, passage_length, passage_upstream)
    adapter_down_matrix, adapter_up_matrix = sent_together(
        (adapter_down_weight, adapter_up_weight), "fsdp", 1, 0
    )
    query_input_rows = query_attention_output[0]
    passage_input_rows = passage_attention_output[0]
    query_rank_rows = jnp.dot(
        query_input_rows, adapter_down_matrix.T, preferred_element_type=jnp.float32
    ).astype(jnp.bfloat16)
    passage_rank_rows = jnp.dot(
        passage_input_rows, adapter_down_matrix.T, preferred_element_type=jnp.float32
    ).astype(jnp.bfloat16)
    up_contribution = ADAPTER_SCALE * (
        jnp.dot(query_rank_rows.T, query_gradient, preferred_element_type=jnp.float32)
        + jnp.dot(passage_rank_rows.T, passage_gradient, preferred_element_type=jnp.float32)
    )
    query_gradient_back = jnp.dot(
        query_gradient, adapter_up_matrix.T, preferred_element_type=jnp.float32
    ).astype(jnp.bfloat16)
    passage_gradient_back = jnp.dot(
        passage_gradient, adapter_up_matrix.T, preferred_element_type=jnp.float32
    ).astype(jnp.bfloat16)
    down_contribution = ADAPTER_SCALE * (
        jnp.dot(query_gradient_back.T, query_input_rows, preferred_element_type=jnp.float32)
        + jnp.dot(passage_gradient_back.T, passage_input_rows, preferred_element_type=jnp.float32)
    )
    down_part, up_part = in_one_piece((down_contribution, up_contribution), "fsdp", 1, 0)
    down_total, up_total = together((down_part, up_part), "dp")
    return (query_gradient[None], passage_gradient[None], down_total, up_total)


def solution(mesh):
    in_specs = (
        P("fsdp", "dp", None),
        P("fsdp", "dp", None),
        P("fsdp", "dp", None),
        P("fsdp", "dp", None),
        P("fsdp", "dp"),
        P("fsdp", "dp", None),
        P("fsdp", None),
        P(None, "fsdp"),
        P(None, "fsdp"),
    )
    out_specs = (P("fsdp", "dp", None), P("fsdp", "dp", None), P(None, "fsdp"), P(None, "fsdp"))
    return jax.shard_map(
        per_device, mesh=mesh, in_specs=in_specs, out_specs=out_specs, check_vma=False
    )
```

profile of v0, /device:TPU:1, one launch (start us, length us, event | category | flops | bytes accessed | tf_op | source)
XLA Modules:
  0.0 227.6 jit_solution(15381119507364947674)
XLA Ops:
  7.2 0.0 all-gather.2.cloned.1.call-start
  7.2 1.1 fusion.19
  8.4 1.6 fusion.2
  10.0 1.5 fusion.63
  11.5 0.6 gather_fusion.2
  12.2 0.9 fusion.18
  13.1 0.0 all-gather.2.cloned.1.call-update
  13.1 0.1 reshape.376
  13.2 6.2 %gather_fusion = s32[1024]{0:T(1024)S(1)} fusion(s32[4096]{0:T(1024)S(1)} %bitcast.127, s32[1024]{0:T(1024)S(1)} %broadcast_clamp_fusion.1), kind=kCustom, calls=%fused_computation | custom fusion | bytes 12288 | tf_op jit(solution)/shard_map/gather | solution.py:92
  19.4 6.0 %scatter_custom_fusion = s32[4096]{0:T(1024)S(1)} fusion(s32[1024]{0:T(1024)S(1)} %bitcast.143, s32[1024]{0:T(1024)S(1)} %broadcast.360, s32[]{:T(128)} %constant.22.clone.1), kind=kCustom, calls=%fused_computation.104 | custom fusion | flops 1024 | bytes 16388 | tf_op jit(solution)/shard_map/scatter-max | solution.py:94
  25.5 0.3 reduce_window_sum.11
  25.8 0.1 multiply_reduce_fusion.2
  25.9 0.1 and_reduce_fusion
  26.0 15.5 %scatter_custom_fusion.1 = s32[256]{0:T(256)S(1)} fusion(s32[4096]{0:T(1024)S(1)} %get-tuple-element.19, s32[4096]{0:T(1024)S(1)} %get-tuple-element.20, s32[]{:T(128)} %constant.22.clone.1), kind=kCustom, calls=%fused_computation.117 | custom fusion | bytes 1028
  41.5 0.1 reshape.370
  41.5 0.1 copy.26
  41.6 16.5 %all_to_all.33 = s32[32,1,8]{2,1,0:T(1,128)S(1)} all-to-all(s32[32,1,8]{2,1,0:T(1,128)S(1)} %copy.26), channel_id=1, replica_groups=mesh['dp'=32,'fsdp'=16] {'dp'}, dimensions={0} | all-to-all | bytes 2048 | tf_op jit(solution)/shard_map/all_to_all | solution.py:108
  58.1 0.1 reshape.400
  58.3 3.2 %gather_fusion.3 = bf16[256,4096]{1,0:T(8,128)(2,1)} fusion(bf16[128,4096]{1,0:T(8,128)(2,1)S(1)} %fusion.63, s32[1024]{0:T(1024)S(1)} %pad_clamp_fusion), kind=kCustom, calls=%fused_computation.3 | custom fusion | bytes 4195328 | tf_op jit(solution)/shard_map/gather | solution.py:109
  61.4 4.3 %all-to-all-start.1 = ((bf16[32,8,4096]{2,1,0:T(8,128)(2,1)}), bf16[32,8,4096]{2,1,0:T(8,128)(2,1)S(1)}, u32[]{:S(2)}, u32[]{:S(2)}) async-start(bf16[32,8,4096]{2,1,0:T(8,128)(2,1)} %bitcast.129), calls=%async_computation.1 | async-start | bytes 4194304 | tf_op jit(solution)/shard_map/all_to_all | solution.py:110
  65.8 0.1 gather.21
  65.8 0.1 reshape.384
  65.9 6.2 %gather_fusion.1 = s32[1024]{0:T(1024)S(1)} fusion(s32[4096]{0:T(1024)S(1)} %add_bitcast_fusion, s32[1024]{0:T(1024)S(1)} %broadcast_clamp_fusion), kind=kCustom, calls=%fused_computation.1 | custom fusion | bytes 12288 | tf_op jit(solution)/shard_map/gather | solution.py:107
  72.1 0.1 gather.25
  72.2 0.1 reshape.383
  72.2 0.1 reshape.375
  72.3 0.1 reshape.406
  72.4 0.5 compare_convert_fusion
  72.9 32.1 %all_gather.7 = bf16[32,4096]{1,0:T(8,128)(2,1)} all-gather(bf16[32,256]{1,0:T(8,128)(2,1)S(1)} %pad_maximum_fusion.2), channel_id=1, replica_groups=mesh['dp'=32,'fsdp'=16] {'fsdp'}, dimensions={1}, use_global_device_ids=true | all-gather | bytes 278528 | tf_op jit(solution)/shard_map/all_gather | solution.py:18
  105.1 0.7 fusion.6
  105.7 8.6 %gather_fusion.4 = f32[1024]{0:T(1024)S(1)} fusion(f32[16,256]{1,0:T(8,128)S(1)} %fusion.6, s32[1024]{0:T(1024)S(1)} %reshape.406), kind=kCustom, calls=%fused_computation.4 | custom fusion | bytes 16384 | tf_op jit(solution)/shard_map/jit(take_along_axis)/gather | solution.py:116
  114.3 0.1 reshape.409
  114.4 0.7 fusion.65
  115.1 0.5 multiply_bitcast_fusion
  115.7 0.7 copy.27
  116.3 0.9 fusion.61
  117.3 0.8 subtract_multiply_fusion
  118.1 0.6 copy-done.10
  118.7 0.1 slice.56
  118.8 1.8 fusion.14
  120.6 1.5 copy.31
  122.0 1.6 reshape.439
  123.6 13.4 %all-to-all-start.2 = ((f32[32,1,128]{2,1,0:T(1,128)}), f32[32,1,128]{2,1,0:T(1,128)}, u32[]{:S(2)}, u32[]{:S(2)}) async-start(f32[32,1,128]{2,1,0:T(1,128)} %reshape.439), calls=%async_computation.2 | async-start | bytes 32768 | tf_op jit(solution)/shard_map/all_to_all | solution.py:150
  137.0 0.8 slice_reduce_fusion
  137.8 2.1 multiply_reduce_fusion.1
  139.9 0.1 divide_convert_fusion.1
  140.1 2.1 fusion.10
  142.2 3.2 %fusion.38 = f32[128,4096]{1,0:T(8,128)} fusion(bf16[16,4096]{1,0:T(8,128)(2,1)} %get-tuple-element.5, f32[16]{0:T(128)} %copy-done.16, s32[16]{0:T(128)} %bitcast.144), kind=kOutput, calls=%fused_computation.58 | convolution fusion | flops 100667392 | bytes 2228352 | tf_op jit(solution)/shard_map/dot_general | solution.py:146
  145.4 1.2 fusion.9
  146.6 0.5 broadcast.414
  147.1 1.4 reduce.9
  148.5 0.1 reshape.440
  148.6 0.5 fusion.28
  149.1 0.0 all-gather.2.cloned.1.call-done
  149.2 5.1 %multiply_reduce_fusion = (f32[128]{0:T(128)S(1)}, f32[128,4096]{1,0:T(8,128)S(1)}) fusion(f32[128]{0:T(128)S(1)} %copy-done.18, bf16[1,128,4096]{2,1,0:T(8,128)(2,1)S(1)} %copy-done.2, f32[128,4096]{1,0:T(8,128)} %fusion.38, f32[128,512]{0,1:T(8,128)S(1)} %bitcast.134, bf16[512,4096]{1,0:T(8,128)(2,1)} %all-gather.2.cloned.1.call-done), kind=kOutput, calls=%fused_computation.20 | convolution fusion | flops 3223846912 | bytes 9700352 | tf_op jit(solution)/shard_map/dot_general | solution.py:163
  154.3 0.5 divide_convert_fusion
  154.8 2.1 fusion
  156.9 0.9 fusion.1
  157.9 29.2 %all_to_all.34 = f32[16,32,256]{2,1,0:T(8,128)S(1)} all-to-all(f32[16,32,256]{2,1,0:T(8,128)S(1)} %bitcast.131), channel_id=1, replica_groups=mesh['dp'=32,'fsdp'=16] {'fsdp'}, dimensions={0} | all-to-all | bytes 1048576 | tf_op jit(solution)/shard_map/all_to_all | solution.py:32
  187.2 0.9 broadcast_in_dim.30
  188.1 30.7 %all_to_all.35 = f32[32,1,8192]{2,1,0:T(1,128)S(1)} all-to-all(f32[32,1,8192]{2,1,0:T(1,128)S(1)} %broadcast_in_dim.30), channel_id=1, replica_groups=mesh['dp'=32,'fsdp'=16] {'dp'}, dimensions={0} | all-to-all | bytes 2097152 | tf_op jit(solution)/shard_map/all_to_all | solution.py:45
  218.8 0.7 reduce_sum.79
  219.5 0.6 slice.43
  220.1 0.6 slice.45
  (73 shorter events, 0.4 us)
Async XLA Ops:
  7.2 147.6 %copy-start = (bf16[1,128,4096]{2,1,0:T(8,128)(2,1)S(1)}, bf16[1,128,4096]{2,1,0:T(8,128)(2,1)}, u32[]{:S(2)}) copy-start(bf16[1,128,4096]{2,1,0:T(8,128)(2,1)} %param.12) | copy-start | bytes 3145732
  7.2 4.3 %copy-start.22 = (s32[1,16]{1,0:T(1,128)S(1)}, s32[1,16]{1,0:T(1,128)}, u32[]{:S(2)}) copy-start(s32[1,16]{1,0:T(1,128)} %param.13) | copy-start | bytes 196
  7.2 142.0 %all-gather.2.cloned.1.call-start = ((), (), s32[]{:S(2)}) async-start(), calls=%async_computation.5 | async-start | bytes 4325376 | tf_op jit(solution)/shard_map/all_gather | solution.py:149
  8.4 96.7 %copy-start.14 = (f32[16]{0:T(128)}, f32[16]{0:T(128)S(1)}, u32[]{:S(2)}) copy-start(f32[16]{0:T(128)S(1)} %add_sqrt_fusion.1) | copy-start | bytes 196
  8.4 3.8 %copy-start.4 = (bf16[1,16,4096]{2,1,0:T(8,128)(2,1)S(1)}, bf16[1,16,4096]{2,1,0:T(8,128)(2,1)}, u32[]{:S(2)}) copy-start(bf16[1,16,4096]{2,1,0:T(8,128)(2,1)} %param.9) | copy-start | bytes 393220
  9.9 3.2 %copy-start.11 = (s32[1,16,64]{2,1,0:T(8,128)S(1)}, s32[1,16,64]{2,1,0:T(8,128)}, u32[]{:S(2)}) copy-start(s32[1,16,64]{2,1,0:T(8,128)} %param.14) | copy-start | bytes 12292
  10.0 3.3 %copy-start.1 = (s32[1,4096]{1,0:T(1,128)S(1)}, s32[1,4096]{1,0:T(1,128)}, u32[]{:S(2)}) copy-start(s32[1,4096]{1,0:T(1,128)} %param.15) | copy-start | bytes 49156
  10.0 1.5 copy-start.17
  12.2 7.2 %copy-start.6 = (bf16[16,4096]{1,0:T(8,128)(2,1)}, bf16[16,4096]{1,0:T(8,128)(2,1)S(1)}, u32[]{:S(2)}) copy-start(bf16[16,4096]{1,0:T(8,128)(2,1)S(1)} %gather_fusion.2) | copy-start | bytes 393220
  13.2 12.6 %copy-start.21 = (s32[2]{0:T(128)S(1)}, s32[2]{0:T(128)}, u32[]{:S(2)}) copy-start(s32[2]{0:T(128)} %constant.80) | copy-start | bytes 28
  13.2 12.7 %copy-start.20 = (s32[2]{0:T(128)S(1)}, s32[2]{0:T(128)}, u32[]{:S(2)}) copy-start(s32[2]{0:T(128)} %constant.83) | copy-start | bytes 28
  61.4 43.6 %all-to-all-start.1 = ((bf16[32,8,4096]{2,1,0:T(8,128)(2,1)}), bf16[32,8,4096]{2,1,0:T(8,128)(2,1)S(1)}, u32[]{:S(2)}, u32[]{:S(2)}) async-start(bf16[32,8,4096]{2,1,0:T(8,128)(2,1)} %bitcast.129), calls=%async_computation.1 | async-start | bytes 4194304 | tf_op jit(solution)/shard_map/all_to_all | solution.py:110
  65.9 7.0 %copy-start.12 = (bf16[16,256]{1,0:T(8,128)(2,1)S(1)}, bf16[16,256]{1,0:T(8,128)(2,1)}, u32[]{:S(2)}) copy-start(bf16[16,256]{1,0:T(8,128)(2,1)} %param.17) | copy-start | bytes 24580
  65.9 7.0 %copy-start.13 = (bf16[16,256]{1,0:T(8,128)(2,1)S(1)}, bf16[16,256]{1,0:T(8,128)(2,1)}, u32[]{:S(2)}) copy-start(bf16[16,256]{1,0:T(8,128)(2,1)} %param.16) | copy-start | bytes 24580
  116.3 23.7 %copy-start.5 = (bf16[32,4096]{1,0:T(8,128)(2,1)S(1)}, bf16[32,4096]{1,0:T(8,128)(2,1)}, u32[]{:S(2)}) copy-start(bf16[32,4096]{1,0:T(8,128)(2,1)} %all_gather.7) | copy-start | bytes 786436
  118.1 0.6 copy-start.10
  123.6 22.9 %all-to-all-start.2 = ((f32[32,1,128]{2,1,0:T(1,128)}), f32[32,1,128]{2,1,0:T(1,128)}, u32[]{:S(2)}, u32[]{:S(2)}) async-start(f32[32,1,128]{2,1,0:T(1,128)} %reshape.439), calls=%async_computation.2 | async-start | bytes 32768 | tf_op jit(solution)/shard_map/all_to_all | solution.py:150
  137.0 2.9 %copy-start.15 = (f32[16]{0:T(128)S(1)}, f32[16]{0:T(128)}, u32[]{:S(2)}) copy-start(f32[16]{0:T(128)} %copy-done.14) | copy-start | bytes 196
  137.8 2.1 copy-start.16
  139.9 5.5 %copy-start.9 = (bf16[1,16,4096]{2,1,0:T(8,128)(2,1)S(1)}, bf16[1,16,4096]{2,1,0:T(8,128)(2,1)}, u32[]{:S(2)}) copy-start(bf16[1,16,4096]{2,1,0:T(8,128)(2,1)} %param.11) | copy-start | bytes 393220
  140.1 14.2 %copy-start.7 = (bf16[16,4096]{1,0:T(8,128)(2,1)}, bf16[16,4096]{1,0:T(8,128)(2,1)S(1)}, u32[]{:S(2)}) copy-start(bf16[16,4096]{1,0:T(8,128)(2,1)S(1)} %divide_convert_fusion.1) | copy-start | bytes 393220
  140.1 9.1 %copy-start.2 = (bf16[1,128,4096]{2,1,0:T(8,128)(2,1)S(1)}, bf16[1,128,4096]{2,1,0:T(8,128)(2,1)}, u32[]{:S(2)}) copy-start(bf16[1,128,4096]{2,1,0:T(8,128)(2,1)} %param.10) | copy-start | bytes 3145732
  140.1 9.1 %copy-start.18 = (f32[128]{0:T(128)S(1)}, f32[128]{0:T(128)}, u32[]{:S(2)}) copy-start(f32[128]{0:T(128)} %copy-done.17) | copy-start | bytes 1540
  149.2 5.1 %copy-start.19 = (f32[128]{0:T(128)S(1)}, f32[128]{0:T(128)}, u32[]{:S(2)}) copy-start(f32[128]{0:T(128)} %copy-done.17) | copy-start | bytes 1540
  154.8 3.0 %copy-start.3 = (bf16[128,4096]{1,0:T(8,128)(2,1)}, bf16[128,4096]{1,0:T(8,128)(2,1)S(1)}, u32[]{:S(2)}) copy-start(bf16[128,4096]{1,0:T(8,128)(2,1)S(1)} %divide_convert_fusion) | copy-start | bytes 3145732
  154.8 2.1 copy-start.8
Sparse Core Ops, SparseCore 0:
  13.2 83.0 all-gather.1
where the time goes:
time: 228 us
  blocking collectives  108 us (47%)
  local copies, waits for them, and re-layouts  49.2 us (22%)
  matrix products  19.6 us (9%)
  other arithmetic  18 us (8%)
  starting transfers between devices  17.7 us (8%)
  between operations  14.6 us (6%)
    all_gather x1, blocking collectives, sent_together(): lax.all_gather(both, axis, axis=dim, tiled=True)  32.1 us
    all_to_all x1, blocking collectives, sent_to_all(): lax.all_to_all(jnp.broadcast_to(array[None], (peers, *array.shape)), axis...  30.7 us
    all_to_all x1, blocking collectives, sum_at_owner(): lax.all_to_all(tiles, axis, split_axis=0, concat_axis=0, tiled=True)  29.2 us
    unnamed x53, local copies, waits for them, and re-layouts  18 us
    all_to_all x1, blocking collectives, per_device(): lax.all_to_all(requests, 'dp', split_axis=0, concat_axis=0, tiled=True)  16.5 us
    all_to_all x1, starting transfers between devices, per_device(): lax.all_to_all(slot_weight.T.reshape(group_size, CAP, slot_weight.shape[0...  13.4 us
    gather x3, local copies, waits for them, and re-layouts, per_device(): negative_scores = jnp.take_along_axis(slot_scores, request_slot, axis=1)  8.74 us
    gather x3, local copies, waits for them, and re-layouts, per_device(): negative_rows = home_rows[hard_negative_ids[0]]  6.29 us
  transfers between devices with their start and end apart: 3, of which 0 were waited for; matrix products, arithmetic and copies ran while one was open for 30% of the time, Pallas kernels for 0%

commit v1 on v0

v1 whole, which is shorter than its diff:
```python
import jax
import jax.numpy as jnp
from jax import lax
from jax.experimental import pallas as pl
from jax.experimental.pallas import tpu as pltpu
from jax.sharding import PartitionSpec as P

MESH = pl.DeviceIdType.MESH
F32, BF16, I32 = jnp.float32, jnp.bfloat16, jnp.int32
HEAT = 100.0
ADAPTER_SCALE = 2.0
EPSILON = 1e-06
D = 4096
H = 2048
T = 512
NN = (((1,), (0,)), ((), ()))
NT = (((1,), (1,)), ((), ()))


def dot(lhs, rhs, dims=NN):
    return lax.dot_general(lhs, rhs, dims, preferred_element_type=F32)


def hi_lo(w):
    hi = w.astype(BF16)
    return hi, (w - hi.astype(F32)).astype(BF16)


def lanes_sum(v):
    return jnp.sum(v, axis=-1, keepdims=True)


def kernel(
    q_ref, p_ref, aq_ref, ap_ref, neg_ref, pos_ref, home_ref, aw_ref, bw_ref,
    gq_ref, gp_ref, res_ref,
    qown, qoth, pb, ab, negp, lhs, rhs, cnt, ssnd, srcv, wsnd, wown, woth,
    t1, rl1, d1p, d1m, r1m, r1p, uf, v1, t2, rl2, d2p, d2m, r2m, r2p,
    pup, dsum, dbuf, drow, rrow, zrow, zbuf, orow, oall,
    ag_s, q_r, qo_r, p_s, p_r, ab_s, ab_r, s_s, s_r, w_s, w_r, wo_s, wo_r,
    rs_s, rs_r, d_s, d_r, rr_s, rr_r, z_s, z_r, o_s, o_r,
):
    dp, z = lax.axis_index("dp"), lax.axis_index("fsdp")
    core, chip = lax.rem(dp, 2), dp // 2
    x, y = chip // 4, lax.rem(chip, 4)
    a = x * (1 - core) + y * core
    b = y * (1 - core) + x * core
    sa, sb = 8 - 6 * core, 2 + 6 * core
    other = 1 - core

    def near(v, k):
        return lax.rem(v + k, 4)

    def at(a_, b_):
        return (a_ * sa + b_ * sb + core, z)

    def slot(a_, b_):
        return b_ * 4 + a_

    me = slot(a, b)
    partner = (chip * 2 + other, z)
    am, a2, ap = near(a, 3), near(a, 2), near(a, 1)
    bm, b2, bp = near(b, 3), near(b, 2), near(b, 1)

    barrier = pltpu.get_barrier_semaphore()

    @pl.loop(1, 32)
    def _(k):
        pl.semaphore_signal(barrier, inc=1, device_id=(lax.rem(dp + k, 32), z), device_id_type=MESH)

    @pl.loop(1, 16)
    def _(k):
        pl.semaphore_signal(barrier, inc=1, device_id=(dp, lax.rem(z + k, 16)), device_id_type=MESH)

    qv = q_ref[...].astype(F32)
    q_len = jnp.sqrt(lanes_sum(qv * qv) + EPSILON)
    qe = (qv * (1.0 / q_len)).astype(BF16)
    qown[me, 0] = qe[:, :H]
    qown[me, 1] = qe[:, H:]

    def p_rows(i, carry):
        rows = pl.ds(pl.multiple_of(i * 32, 32), 32)
        pv = p_ref[rows, :].astype(F32)
        p_len = jnp.sqrt(lanes_sum(pv * pv) + EPSILON)
        dst = pl.ds(pl.multiple_of(core * 128 + i * 32, 32), 32)
        pb[dst, :] = (pv * (1.0 / p_len)).astype(BF16)
        return carry

    lax.fori_loop(0, 4, p_rows, 0)
    zcols = pl.ds(pl.multiple_of(z * 256, 256), 256)
    ab[0:16, zcols] = aw_ref[...]
    ab[16:32, zcols] = bw_ref[...]

    pl.semaphore_wait(barrier, 46)

    sent = []

    def push(src, dst, ssem, rsem, device):
        c = pltpu.make_async_remote_copy(
            src_ref=src, dst_ref=dst, send_sem=ssem, recv_sem=rsem, device_id=device, device_id_type=MESH
        )
        c.start()
        return c

    def arrive(dst, rsem, ssem):
        pltpu.make_async_remote_copy(
            src_ref=dst, dst_ref=dst, send_sem=ssem, recv_sem=rsem, device_id=partner, device_id_type=MESH
        ).wait_recv()

    def gone(src, ssem, rsem):
        pltpu.make_async_remote_copy(
            src_ref=src, dst_ref=src, send_sem=ssem, recv_sem=rsem, device_id=partner, device_id_type=MESH
        ).wait_send()

    def q_full(s, device):
        n = len(sent)
        sent.append(push(qown.at[s], qown.at[s], ag_s.at[n], q_r.at[s, 0], device))

    def q_half(s, h, device):
        n = len(sent)
        sent.append(push(qown.at[s, h], qown.at[s, h], ag_s.at[n], q_r.at[s, h], device))

    def q_other(s):
        n = len(sent)
        sent.append(push(qown.at[s], qoth.at[s], ag_s.at[n], qo_r.at[s], partner))

    def got_full(s):
        arrive(qown.at[s], q_r.at[s, 0], ag_s.at[0])

    def got_halves(s):
        arrive(qown.at[s, 0], q_r.at[s, 0], ag_s.at[0])
        arrive(qown.at[s, 1], q_r.at[s, 1], ag_s.at[0])

    q_full(me, at(ap, b))
    q_full(me, at(am, b))
    q_full(me, at(a, bp))
    q_full(me, at(a, bm))
    own_rows = pl.ds(pl.multiple_of(core * 128, 128), 128)
    other_rows = pl.ds(pl.multiple_of(other * 128, 128), 128)
    p_copy = push(pb.at[own_rows], pb.at[own_rows], p_s, p_r, partner)
    q_other(me)

    @pl.loop(1, 16)
    def _(k):
        push(ab.at[:, zcols], ab.at[:, zcols], ab_s.at[k], ab_r.at[z], (dp, lax.rem(z + k, 16)))

    negp[...] = jnp.full((16, 128), -1, I32)
    negp[:, 0:64] = neg_ref[...]
    n_row = jnp.concatenate([negp[k : k + 1, :] for k in range(16)], axis=1)
    home = home_ref[...]
    table = jnp.concatenate(
        [(home >> 7).astype(F32).T, (home & 127).astype(F32).T], axis=0
    ).astype(BF16)
    for part in range(4):
        n = n_row[:, part * T : (part + 1) * T]
        lane_q = (lax.broadcasted_iota(I32, (1, T), 1) >> 7) + part * 4
        picked = (lax.broadcasted_iota(I32, (32, T), 0) == (n >> 7)).astype(F32).astype(BF16)
        found = dot(table, picked)
        low = lax.broadcasted_iota(I32, (128, T), 0) == (n & 127)
        dev_row = jnp.sum(jnp.where(low, found[0:128], 0.0), axis=0, keepdims=True).astype(I32)
        in_dev = jnp.sum(jnp.where(low, found[128:256], 0.0), axis=0, keepdims=True).astype(I32)
        chip_row = dev_row >> 1
        key = ((chip_row >> 2) * (1 + 3 * core) + (chip_row & 3) * (4 - 3 * core)) * 16 + lane_q
        key = jnp.where(n >= 0, key, -1)
        col = (dev_row & 1) * 128 + in_dev
        rows = lax.broadcasted_iota(I32, (256, T), 0)
        lhs[:, part * T : (part + 1) * T] = (rows == key).astype(F32).astype(BF16)
        rhs[:, part * T : (part + 1) * T] = (rows == col).astype(F32).astype(BF16)
    times = dot(lhs[...], rhs[...], NT)
    cnt[:, 0] = times[:, 0:128].reshape(16, 16, 128)
    cnt[:, 1] = times[:, 128:256].reshape(16, 16, 128)
    pos = jnp.zeros((16, 128), I32)
    for k in range(16):
        pos = jnp.where(lax.broadcasted_iota(I32, (16, 128), 0) == k, pos_ref[0, k], pos)
    is_pos = (lax.broadcasted_iota(I32, (16, 128), 1) == pos).astype(F32)
    cnt[me, core] = cnt[me, core] + is_pos

    def scores(b_):
        block = pl.ds(b_ * 4, 4)
        s = dot(qown[block, 0].reshape(64, H), pb[:, 0:H], NT)
        s = (s + dot(qown[block, 1].reshape(64, H), pb[:, H:D], NT)) * HEAT
        ssnd[block, 0] = s[:, 0:128].reshape(4, 16, 128)
        ssnd[block, 1] = s[:, 128:256].reshape(4, 16, 128)

    def send_scores(b_, skip_own):
        for i in range(4):
            if skip_own and i == 0:
                continue
            a_ = near(a, i)
            s = slot(a_, b_)
            push(ssnd.at[s], srcv.at[me], s_s.at[s], s_r.at[me], at(a_, b_))

    got_full(slot(am, b))
    q_half(slot(am, b), 0, at(ap, b))
    q_full(slot(am, b), at(a, bp))
    q_full(slot(am, b), at(a, bm))
    got_full(slot(ap, b))
    q_half(slot(ap, b), 1, at(am, b))
    q_full(slot(ap, b), at(a, bp))
    q_full(slot(ap, b), at(a, bm))
    q_other(slot(am, b))
    q_other(slot(ap, b))
    got_full(slot(a, bm))
    q_half(slot(a, bm), 0, at(a, bp))
    got_full(slot(a, bp))
    q_half(slot(a, bp), 1, at(a, bm))
    got_halves(slot(a2, b))
    q_full(slot(a2, b), at(a, bp))
    q_full(slot(a2, b), at(a, bm))
    q_other(slot(a2, b))
    q_other(slot(a, bm))
    q_other(slot(a, bp))
    arrive(pb.at[other_rows], p_r, p_s)
    scores(b)
    send_scores(b, True)
    srcv[me] = ssnd[me]
    for a_ in (am, ap, a2):
        got_full(slot(a_, bm))
        q_half(slot(a_, bm), 0, at(a, bp))
        got_full(slot(a_, bp))
        q_half(slot(a_, bp), 1, at(a, bm))
        q_other(slot(a_, bm))
        q_other(slot(a_, bp))
    scores(bm)
    send_scores(bm, False)
    scores(bp)
    send_scores(bp, False)
    for a_ in (a, am, ap, a2):
        got_halves(slot(a_, b2))
    scores(b2)
    send_scores(b2, False)
    for a_ in (a, am, ap, a2):
        q_other(slot(a_, b2))

    @pl.loop(1, 16)
    def _(k):
        zk = lax.rem(z + k, 16)
        cols = pl.ds(pl.multiple_of(zk * 256, 256), 256)
        arrive(ab.at[:, cols], ab_r.at[zk], ab_s.at[1])

    low_p = dot(ab[0:16, :], ap_ref[...], NT).astype(BF16)
    low_q = dot(ab[0:16, :], aq_ref[...], NT).astype(BF16)

    def peers(body):
        @pl.loop(1, 16)
        def _(k):
            a_, b_ = near(a, lax.rem(k, 4)), near(b, k // 4)
            body(a_, b_, slot(a_, b_))

    peers(lambda a_, b_, s: arrive(srcv.at[s], s_r.at[s], s_s.at[0]))

    low_value = jnp.full((16, 128), -1e30, F32)

    def top_of(s, m):
        m = jnp.maximum(m, jnp.where(cnt[s, 0] > 0.0, srcv[s, 0], low_value))
        return jnp.maximum(m, jnp.where(cnt[s, 1] > 0.0, srcv[s, 1], low_value))

    top = low_value
    for s in range(16):
        top = top_of(s, top)
    top = jnp.max(top, axis=-1, keepdims=True)
    total = jnp.zeros((16, 128), F32)
    for s in range(16):
        for k in range(2):
            c = cnt[s, k]
            e = c * jnp.exp(jnp.where(c > 0.0, srcv[s, k] - top, low_value))
            wsnd[s, k] = e
            total = total + e
    scale = HEAT / lanes_sum(total)
    for s in range(16):
        for k in range(2):
            wsnd[s, k] = wsnd[s, k] * scale
    wsnd[me, core] = wsnd[me, core] - HEAT * is_pos

    peers(lambda a_, b_, s: push(wsnd.at[s], wown.at[me], w_s.at[s], w_r.at[me], at(a_, b_)))

    @pl.loop(0, 16)
    def _(k):
        a_, b_ = near(a, lax.rem(k, 4)), near(b, k // 4)
        s = slot(a_, b_)
        push(wsnd.at[s, other], woth.at[me], wo_s.at[s], wo_r.at[me], (a_ * sa + b_ * sb + other, z))

    wown[me] = wsnd[me]
    peers(lambda a_, b_, s: arrive(wown.at[s], w_r.at[s], w_s.at[0]))

    def shares(b_, h, put):
        block = pl.ds(b_ * 4, 4)
        w = jnp.concatenate([wown[block, 0].reshape(64, 128), wown[block, 1].reshape(64, 128)], axis=1)
        w = jnp.concatenate(hi_lo(w), axis=0)
        for j in range(H // T):
            r = dot(w, pb[:, h * H + j * T : h * H + (j + 1) * T])
            put(slice(j * T, (j + 1) * T), (r[0:64] + r[64:128]).reshape(4, 16, T))

    def put_in(ref, *where):
        def put(cols, r):
            ref[(*where, slice(None), slice(None), cols)] = r.astype(ref.dtype)

        return put

    rs = []

    def hop(src, dst, device):
        n = len(rs)
        rs.append(push(src, dst, rs_s.at[n], rs_r.at[n], device))

    def landed(dst, n):
        arrive(dst, rs_r.at[n], rs_s.at[0])

    shares(b2, 0, put_in(t1, 0))
    hop(t1.at[0], rl1.at[0], at(a, bp))
    shares(b2, 1, put_in(t1, 1))
    hop(t1.at[1], rl1.at[1], at(a, bm))
    shares(bp, 1, put_in(d1p, 1))
    hop(d1p.at[1], r1m.at[1], at(a, bp))
    shares(bm, 0, put_in(d1m, 0))
    hop(d1m.at[0], r1p.at[0], at(a, bm))
    shares(bp, 0, put_in(uf, 0))
    shares(bm, 1, put_in(uf, 1))
    landed(rl1.at[0], 0)
    d1p[0] = (uf[0] + rl1[0].astype(F32)).astype(BF16)
    hop(d1p.at[0], r1m.at[0], at(a, bp))
    landed(rl1.at[1], 1)
    d1m[1] = (uf[1] + rl1[1].astype(F32)).astype(BF16)
    hop(d1m.at[1], r1p.at[1], at(a, bm))
    shares(b, 0, put_in(v1, 0))
    shares(b, 1, put_in(v1, 1))

    for a_, b_ in ((am, b), (ap, b), (a2, b), (a, bm), (a, bp), (a, b)):
        arrive(qoth.at[slot(a_, b_)], qo_r.at[slot(a_, b_)], ag_s.at[0])
    for a_ in (am, ap, a2):
        for b_ in (bm, bp):
            arrive(qoth.at[slot(a_, b_)], qo_r.at[slot(a_, b_)], ag_s.at[0])
    for a_ in (a, am, ap, a2):
        arrive(qoth.at[slot(a_, b2)], qo_r.at[slot(a_, b2)], ag_s.at[0])

    @pl.loop(0, 16)
    def _(s):
        arrive(woth.at[s], wo_r.at[s], wo_s.at[0])

    wt = jnp.concatenate([wown[:, core].reshape(256, 128).T, woth[...].reshape(256, 128).T], axis=1)
    wt = jnp.concatenate(hi_lo(wt), axis=0)
    p_sq = jnp.zeros((128, 1), F32)
    p_in = jnp.zeros((128, 1), F32)
    for h in range(2):
        for j in range(H // T):
            cols = slice(h * H + j * T, h * H + (j + 1) * T)
            sub = slice(j * T, (j + 1) * T)
            r = dot(wt[:, 0:256], qown[:, h, :, sub].reshape(256, T))
            r = r + dot(wt[:, 256:512], qoth[:, h, :, sub].reshape(256, T))
            r = r[0:128] + r[128:256]
            pv = p_ref[:, cols].astype(F32)
            p_sq = p_sq + lanes_sum(pv * pv)
            p_in = p_in + lanes_sum(pv * r)
            pup[:, cols] = r
    p_inv = 1.0 / jnp.sqrt(p_sq + EPSILON)
    p_in = p_in * p_inv * p_inv
    for j in range(D // T):
        cols = slice(j * T, (j + 1) * T)
        gp_ref[:, cols] = ((pup[:, cols] - p_ref[:, cols].astype(F32) * p_in) * p_inv).astype(BF16)

    landed(r1m.at[1], 2)
    landed(r1p.at[0], 3)
    landed(r1m.at[0], 4)
    landed(r1p.at[1], 5)
    for h in range(2):
        v1[h] = v1[h] + r1m[h].astype(F32) + r1p[h].astype(F32)
        t2[h] = v1[h, a2].astype(BF16)
        if h == 0:
            hop(t2.at[0], rl2.at[0], at(ap, b))
            d2m[0] = v1[0, am].astype(BF16)
            hop(d2m.at[0], r2p.at[0], at(am, b))
        else:
            hop(t2.at[1], rl2.at[1], at(am, b))
            d2p[1] = v1[1, ap].astype(BF16)
            hop(d2p.at[1], r2m.at[1], at(ap, b))
    landed(rl2.at[0], 6)
    d2p[0] = (v1[0, ap] + rl2[0].astype(F32)).astype(BF16)
    hop(d2p.at[0], r2m.at[0], at(ap, b))
    landed(rl2.at[1], 8)
    d2m[1] = (v1[1, am] + rl2[1].astype(F32)).astype(BF16)
    hop(d2m.at[1], r2p.at[1], at(am, b))

    back_p = dot(ab[16:32, :], gp_ref[...], NT).astype(BF16)
    for j in range(D // T):
        cols = slice(j * T, (j + 1) * T)
        dsum[0:16, cols] = dot(back_p, ap_ref[:, cols])
        dsum[16:32, cols] = dot(low_p, gp_ref[:, cols])

    landed(r2p.at[0], 7)
    landed(r2m.at[1], 9)
    landed(r2m.at[0], 10)
    landed(r2p.at[1], 11)
    qu = jnp.concatenate(
        [v1[h, a] + r2m[h].astype(F32) + r2p[h].astype(F32) for h in range(2)], axis=1
    )
    qv = q_ref[...].astype(F32)
    q_inv = 1.0 / jnp.sqrt(lanes_sum(qv * qv) + EPSILON)
    q_in = lanes_sum(qv * qu) * q_inv * q_inv
    gq = ((qu - qv * q_in) * q_inv).astype(BF16)
    gq_ref[...] = gq
    back_q = dot(ab[16:32, :], gq, NT).astype(BF16)
    for j in range(D // T):
        cols = slice(j * T, (j + 1) * T)
        dsum[0:16, cols] = ADAPTER_SCALE * (dsum[0:16, cols] + dot(back_q, aq_ref[:, cols]))
        dsum[16:32, cols] = ADAPTER_SCALE * (dsum[16:32, cols] + dot(low_q, gq[:, cols]))

    mine = pl.ds(pl.multiple_of(core * 16, 16), 16)
    theirs = pl.ds(pl.multiple_of(other * 16, 16), 16)
    d_copy = push(dsum.at[theirs], dbuf, d_s, d_r, partner)
    arrive(dbuf, d_r, d_s)
    for j in range(D // 128):
        cols = slice(j * 128, (j + 1) * 128)
        drow[:, j // 2, j % 2, :] = dsum[mine, cols] + dbuf[:, cols]
    peers(lambda a_, b_, s: push(drow.at[s], rrow.at[me], rr_s.at[s], rr_r.at[me], at(a_, b_)))
    rrow[me] = drow[me]
    peers(lambda a_, b_, s: arrive(rrow.at[s], rr_r.at[s], rr_s.at[0]))
    acc = rrow[0]
    for s in range(1, 16):
        acc = acc + rrow[s]
    zrow[...] = acc

    @pl.loop(1, 16)
    def _(k):
        zk = lax.rem(z + k, 16)
        push(zrow.at[zk], zbuf.at[z], z_s.at[zk], z_r.at[z], (dp, zk))

    zbuf[z] = zrow[z]

    @pl.loop(1, 16)
    def _(k):
        zk = lax.rem(z + k, 16)
        arrive(zbuf.at[zk], z_r.at[zk], z_s.at[0])

    acc = zbuf[0]
    for s in range(1, 16):
        acc = acc + zbuf[s]
    orow[...] = acc
    oall[core, me] = acc

    @pl.loop(1, 32)
    def _(k):
        push(orow, oall.at[core, me], o_s.at[k], o_r.at[core, me], (lax.rem(dp + k, 32), z))

    @pl.loop(1, 32)
    def _(k):
        d_ = lax.rem(dp + k, 32)
        c_, h_ = lax.rem(d_, 2), d_ // 2
        s_ = (h_ // 4) * (1 + 3 * c_) + lax.rem(h_, 4) * (4 - 3 * c_)
        arrive(oall.at[c_, s_], o_r.at[c_, s_], o_s.at[1])

    res_ref[...] = oall[...]

    for c in sent + rs + [p_copy, d_copy]:
        c.wait_send()

    @pl.loop(1, 16)
    def _(k):
        a_, b_ = near(a, lax.rem(k, 4)), near(b, k // 4)
        s = slot(a_, b_)
        gone(ssnd.at[s], s_s.at[s], s_r.at[s])
        gone(wsnd.at[s], w_s.at[s], w_r.at[s])
        gone(drow.at[s], rr_s.at[s], rr_r.at[s])
        zk = lax.rem(z + k, 16)
        gone(zrow.at[zk], z_s.at[zk], z_r.at[zk])
        gone(ab.at[:, zcols], ab_s.at[k], ab_r.at[z])

    @pl.loop(0, 16)
    def _(k):
        gone(wsnd.at[k, other], wo_s.at[k], wo_r.at[k])

    @pl.loop(1, 32)
    def _(k):
        gone(orow, o_s.at[k], o_r.at[0, 0])


VM = pl.BlockSpec(memory_space=pltpu.VMEM)
SM = pl.BlockSpec(memory_space=pltpu.SMEM)


def per_device(query, passage, query_attn, passage_attn, positives, negatives, home, down, up):
    block = (16, 2, 16, 128)
    dma = pltpu.SemaphoreType.DMA
    grad_q, grad_p, res = pl.pallas_call(
        kernel,
        out_shape=(
            jax.ShapeDtypeStruct((16, D), BF16),
            jax.ShapeDtypeStruct((128, D), BF16),
            jax.ShapeDtypeStruct((2, 16, 2, 128), F32),
        ),
        in_specs=[VM, VM, VM, VM, VM, SM, VM, VM, VM],
        out_specs=(VM, VM, VM),
        scratch_shapes=[
            pltpu.VMEM((16, 2, 16, H), BF16),
            pltpu.VMEM((16, 2, 16, H), BF16),
            pltpu.VMEM((256, D), BF16),
            pltpu.VMEM((32, D), BF16),
            pltpu.VMEM((16, 128), I32),
            pltpu.VMEM((256, H), BF16),
            pltpu.VMEM((256, H), BF16),
            pltpu.VMEM(block, F32),
            pltpu.VMEM(block, F32),
            pltpu.VMEM(block, F32),
            pltpu.VMEM(block, F32),
            pltpu.VMEM(block, F32),
            pltpu.VMEM((16, 16, 128), F32),
            pltpu.VMEM((2, 4, 16, H), BF16),
            pltpu.VMEM((2, 4, 16, H), BF16),
            pltpu.VMEM((2, 4, 16, H), BF16),
            pltpu.VMEM((2, 4, 16, H), BF16),
            pltpu.VMEM((2, 4, 16, H), BF16),
            pltpu.VMEM((2, 4, 16, H), BF16),
            pltpu.VMEM((2, 4, 16, H), F32),
            pltpu.VMEM((2, 4, 16, H), F32),
            pltpu.VMEM((2, 16, H), BF16),
            pltpu.VMEM((2, 16, H), BF16),
            pltpu.VMEM((2, 16, H), BF16),
            pltpu.VMEM((2, 16, H), BF16),
            pltpu.VMEM((2, 16, H), BF16),
            pltpu.VMEM((2, 16, H), BF16),
            pltpu.VMEM((128, D), F32),
            pltpu.VMEM((32, D), F32),
            pltpu.VMEM((16, D), F32),
            pltpu.VMEM((16, 16, 2, 128), F32),
            pltpu.VMEM((16, 16, 2, 128), F32),
            pltpu.VMEM((16, 2, 128), F32),
            pltpu.VMEM((16, 2, 128), F32),
            pltpu.VMEM((2, 128), F32),
            pltpu.VMEM((2, 16, 2, 128), F32),
            dma((40,)),
            dma((16, 2)),
            dma((16,)),
            dma(()),
            dma(()),
            dma((16,)),
            dma((16,)),
            dma((16,)),
            dma((16,)),
            dma((16,)),
            dma((16,)),
            dma((16,)),
            dma((16,)),
            dma((12,)),
            dma((12,)),
            dma(()),
            dma(()),
            dma((16,)),
            dma((16,)),
            dma((16,)),
            dma((16,)),
            dma((32,)),
            dma((2, 16)),
        ],
        compiler_params=pltpu.CompilerParams(
            collective_id=0, has_side_effects=True, vmem_limit_bytes=60 * 1024 * 1024
        ),
    )(
        query[0], passage[0], query_attn[0], passage_attn[0], negatives[0], positives,
        home[0].reshape(32, 128), down, up,
    )
    sums = res.reshape(2, 16, 256)
    return grad_q[None], grad_p[None], sums[0], sums[1]


def solution(mesh):
    in_specs = (
        P("fsdp", "dp", None),
        P("fsdp", "dp", None),
        P("fsdp", "dp", None),
        P("fsdp", "dp", None),
        P("fsdp", "dp"),
        P("fsdp", "dp", None),
        P("fsdp", None),
        P(None, "fsdp"),
        P(None, "fsdp"),
    )
    out_specs = (P("fsdp", "dp", None), P("fsdp", "dp", None), P(None, "fsdp"), P(None, "fsdp"))
    return jax.shard_map(
        per_device, mesh=mesh, in_specs=in_specs, out_specs=out_specs, check_vma=False
    )
```

time: 228 us -> 101 us (0.44)
  blocking collectives: 108 us -> 0 us
  Pallas kernels: 0 us -> 95.5 us
  local copies, waits for them, and re-layouts: 49.2 us -> 4.33 us
  matrix products: 19.6 us -> 0 us
  other arithmetic: 18 us -> 0 us
  starting transfers between devices: 17.7 us -> 0 us
  between operations: 14.6 us -> 0.65 us
    pallas_call x0 -> x1, Pallas kernels: none -> 95.5 us  [per_device(): pl.pallas_call(kernel, out_shape=(jax.ShapeDtypeStruct((16, D), BF16), ja...]
    all_to_all x3 -> x0, blocking collectives: 76.3 us -> none  [the longest x1 30.7 us: sent_to_all(): lax.all_to_all(jnp.broadcast_to(array[None], (peers, *array.shape)), axis...]
    all_gather x1 -> x0, blocking collectives: 32.1 us -> none  [sent_together(): lax.all_gather(both, axis, axis=dim, tiled=True)]
    gather x11 -> x0, local copies, waits for them, and re-layouts: 25.1 us -> none  [the longest x3 8.74 us: per_device(): negative_scores = jnp.take_along_axis(slot_scores, request_slot, axis=1)]
    dot_general x10 -> x0, matrix products: 19.6 us -> none  [the longest x1 5.1 us: per_device(): jnp.dot(owner_weight, gathered_queries.astype(jnp.float32), precision=lax...]
    all_to_all x2 -> x0, starting transfers between devices: 17.7 us -> none  [the longest x1 13.4 us: per_device(): lax.all_to_all(slot_weight.T.reshape(group_size, CAP, slot_weight.shape[0...]
    unnamed x53 -> x4, local copies, waits for them, and re-layouts: 18 us -> 2.95 us
    another operation x2 -> x0, other arithmetic: 6.33 us -> none  [the longest x1 6.04 us: per_device(): jnp.zeros((group_size * P_DEV,), jnp.int32).at[negative_rows.reshape(-1)]]
  transfers between devices with their start and end apart: 3 -> 0, of which waited for: 0 -> 0; matrix products, arithmetic and copies ran while one was open for 30% -> 0% of each run, Pallas kernels for 0% -> 0%
where the time goes in v1:
time: 101 us
  Pallas kernels  95.5 us (95%)
  local copies, waits for them, and re-layouts  4.33 us (4%)
    pallas_call x1, Pallas kernels, per_device(): pl.pallas_call(kernel, out_shape=(jax.ShapeDtypeStruct((16, D), BF16), ja...  95.5 us
    unnamed x4, local copies, waits for them, and re-layouts  2.95 us

profile of v1, /device:TPU:1, one launch (start us, length us, event | category | flops | bytes accessed | tf_op | source)
XLA Modules:
  0.0 100.5 jit_solution(12950730774642871095)
XLA Ops:
  0.6 95.5 %shard_map.120 = (bf16[16,4096]{1,0:T(8,128)(2,1)}, bf16[128,4096]{1,0:T(8,128)(2,1)}, f32[2,16,2,128]{3,2,1,0:T(2,128)}) custom-call(bf16[16,4096]{1,0:T(8,128)(2,1)} %bitcast.20, bf16[128,4096]{1,0:T(8,128)(2,1)} %bitcast.17, bf16[16,4096]{1,0:T(8,128)(2,1)} %bitcast.21, bf16[128,4096]{1,0:T(8,128)(2,1)} %bitcast.18, s32[16,64]{1,0:T(8,128)} %bitcast.25, ...), custom_call_target="tpu_custom_call" | custom-call | tf_op jit(solution)/shard_map/pallas_call | solution.py:482
  96.2 0.0 copy-start
  96.2 0.8 fusion
  97.0 0.6 copy_bitcast_fusion
  97.6 0.0 copy-done
  97.6 0.7 copy.19
  98.2 2.3 %copy.20 = bf16[1,128,4096]{2,1,0:T(8,128)(2,1)} copy(bf16[1,128,4096]{2,1,0:T(8,128)(2,1)} %bitcast.16) | data formatting | bytes 2097152
Async XLA Ops:
  96.2 1.4 %copy-start = (bf16[16,4096]{1,0:T(8,128)(2,1)S(1)}, bf16[16,4096]{1,0:T(8,128)(2,1)}, u32[]{:S(2)}) copy-start(bf16[16,4096]{1,0:T(8,128)(2,1)} %get-tuple-element.7) | copy-start | bytes 393220

commit v2 on v1

v2 whole, which is shorter than its diff:
```python
import jax
import jax.numpy as jnp
from jax import lax
from jax.experimental import pallas as pl
from jax.experimental.pallas import tpu as pltpu
from jax.sharding import PartitionSpec as P

MESH = pl.DeviceIdType.MESH
F32, BF16, I32 = jnp.float32, jnp.bfloat16, jnp.int32
HEAT = 100.0
ADAPTER_SCALE = 2.0
EPSILON = 1e-06
D = 4096
H = 2048
T = 512
NN = (((1,), (0,)), ((), ()))
NT = (((1,), (1,)), ((), ()))


def dot(lhs, rhs, dims=NN):
    return lax.dot_general(lhs, rhs, dims, preferred_element_type=F32)


def hi_lo(w):
    hi = w.astype(BF16)
    return hi, (w - hi.astype(F32)).astype(BF16)


def lanes_sum(v):
    return jnp.sum(v, axis=-1, keepdims=True)


def kernel(
    q_hbm, p_hbm, aq_hbm, ap_hbm, neg_hbm, home_hbm, aw_hbm, bw_hbm, pos_ref,
    gq_hbm, gp_hbm, down_hbm, up_hbm,
    q_ref, p_ref, aq_ref, ap_ref, neg_ref, home_ref, aw_ref, bw_ref, gq_ref, gp_ref, dv,
    qown, qoth, pb, ab, negp, lhs, rhs, csnd, crcv, ct, est, stat, srcv, rows_s,
    wt, woth, wq, gsnd, grcv, ysnd, yrcv,
    t1, rl1, d1p, d1m, r1m, r1p, uf, v1, t2, rl2, d2p, d2m, r2m, r2p,
    pup, dsum, dbuf, drow, rrow, zrow, zbuf, orow, oall,
    in_s, out_s, ag_s, q_r, qo_r, p_s, p_r, ab_s, ab_r, c_s, c_r, s_s, s_r, w_s, w_r, g_s, g_r, y_s, y_r,
    rs_s, rs_r, d_s, d_r, rr_s, rr_r, z_s, z_r, o_s, o_r,
):
    dp, z = lax.axis_index("dp"), lax.axis_index("fsdp")
    core, chip = lax.rem(dp, 2), dp // 2
    x, y = chip // 4, lax.rem(chip, 4)
    a = x * (1 - core) + y * core
    b = y * (1 - core) + x * core
    sa, sb = 8 - 6 * core, 2 + 6 * core
    other = 1 - core

    def near(v, k):
        return lax.rem(v + k, 4)

    def at(a_, b_):
        return (a_ * sa + b_ * sb + core, z)

    def slot(a_, b_):
        return b_ * 4 + a_

    me = slot(a, b)
    partner = (chip * 2 + other, z)
    am, a2, ap = near(a, 3), near(a, 2), near(a, 1)
    bm, b2, bp = near(b, 3), near(b, 2), near(b, 1)

    barrier = pltpu.get_barrier_semaphore()

    @pl.loop(1, 32)
    def _(k):
        pl.semaphore_signal(barrier, inc=1, device_id=(lax.rem(dp + k, 32), z), device_id_type=MESH)

    @pl.loop(1, 16)
    def _(k):
        pl.semaphore_signal(barrier, inc=1, device_id=(dp, lax.rem(z + k, 16)), device_id_type=MESH)

    loads = [
        pltpu.make_async_copy(src, dst, in_s.at[i])
        for i, (src, dst) in enumerate(
            (
                (q_hbm, q_ref), (p_hbm, p_ref), (aw_hbm, aw_ref), (bw_hbm, bw_ref),
                (neg_hbm, neg_ref), (home_hbm, home_ref), (aq_hbm, aq_ref), (ap_hbm, ap_ref),
            )
        )
    ]
    for c in loads:
        c.start()

    loads[0].wait()
    qv = q_ref[...].astype(F32)
    q_inv = 1.0 / jnp.sqrt(lanes_sum(qv * qv) + EPSILON)
    qe = (qv * q_inv).astype(BF16)
    qown[me, 0] = qe[:, :H]
    qown[me, 1] = qe[:, H:]
    for i in (2, 3):
        loads[i].wait()
    zcols = pl.ds(pl.multiple_of(z * 256, 256), 256)
    ab[0:16, zcols] = aw_ref[...]
    ab[16:32, zcols] = bw_ref[...]
    loads[1].wait()

    def p_rows(i, carry):
        rows = pl.ds(pl.multiple_of(i * 32, 32), 32)
        pv = p_ref[rows, :].astype(F32)
        p_len = jnp.sqrt(lanes_sum(pv * pv) + EPSILON)
        dst = pl.ds(pl.multiple_of(core * 128 + i * 32, 32), 32)
        pb[dst, :] = (pv * (1.0 / p_len)).astype(BF16)
        return carry

    lax.fori_loop(0, 4, p_rows, 0)

    pl.semaphore_wait(barrier, 46)

    sent = []

    def push(src, dst, ssem, rsem, device):
        c = pltpu.make_async_remote_copy(
            src_ref=src, dst_ref=dst, send_sem=ssem, recv_sem=rsem, device_id=device, device_id_type=MESH
        )
        c.start()
        return c

    def arrive(dst, rsem, ssem):
        pltpu.make_async_remote_copy(
            src_ref=dst, dst_ref=dst, send_sem=ssem, recv_sem=rsem, device_id=partner, device_id_type=MESH
        ).wait_recv()

    def gone(src, ssem, rsem):
        pltpu.make_async_remote_copy(
            src_ref=src, dst_ref=src, send_sem=ssem, recv_sem=rsem, device_id=partner, device_id_type=MESH
        ).wait_send()

    def peers(body):
        def one(k):
            a_, b_ = near(a, lax.rem(6 - lax.rem(k, 4), 4)), near(b, lax.rem(6 - k // 4, 4))
            body(a_, b_, slot(a_, b_))

        pl.loop(0, 10)(one)
        pl.loop(11, 16)(one)

    def q_full(s, device):
        n = len(sent)
        sent.append(push(qown.at[s], qown.at[s], ag_s.at[n], q_r.at[s, 0], device))

    def q_half(s, h, device):
        n = len(sent)
        sent.append(push(qown.at[s, h], qown.at[s, h], ag_s.at[n], q_r.at[s, h], device))

    def q_other(s):
        n = len(sent)
        sent.append(push(qown.at[s], qoth.at[s], ag_s.at[n], qo_r.at[s], partner))

    def got_full(s):
        arrive(qown.at[s], q_r.at[s, 0], ag_s.at[0])

    def got_halves(s):
        arrive(qown.at[s, 0], q_r.at[s, 0], ag_s.at[0])
        arrive(qown.at[s, 1], q_r.at[s, 1], ag_s.at[0])

    q_full(me, at(ap, b))
    q_full(me, at(am, b))
    q_full(me, at(a, bp))
    q_full(me, at(a, bm))
    own_rows = pl.ds(pl.multiple_of(core * 128, 128), 128)
    other_rows = pl.ds(pl.multiple_of(other * 128, 128), 128)
    p_copy = push(pb.at[own_rows], pb.at[own_rows], p_s, p_r, partner)
    q_other(me)

    @pl.loop(1, 16)
    def _(k):
        push(ab.at[:, zcols], ab.at[:, zcols], ab_s.at[k], ab_r.at[z], (dp, lax.rem(z + k, 16)))

    loads[4].wait()
    loads[5].wait()
    negp[...] = jnp.full((16, 128), -1, I32)
    negp[:, 0:64] = neg_ref[...]
    n_row = jnp.concatenate([negp[k : k + 1, :] for k in range(16)], axis=1)
    home = home_ref[...]
    table = jnp.concatenate(
        [(home >> 7).astype(F32).T, (home & 127).astype(F32).T], axis=0
    ).astype(BF16)
    for part in range(4):
        n = n_row[:, part * T : (part + 1) * T]
        lane_q = (lax.broadcasted_iota(I32, (1, T), 1) >> 7) + part * 4
        picked = (lax.broadcasted_iota(I32, (32, T), 0) == (n >> 7)).astype(F32).astype(BF16)
        found = dot(table, picked)
        low = lax.broadcasted_iota(I32, (128, T), 0) == (n & 127)
        dev_row = jnp.sum(jnp.where(low, found[0:128], 0.0), axis=0, keepdims=True).astype(I32)
        in_dev = jnp.sum(jnp.where(low, found[128:256], 0.0), axis=0, keepdims=True).astype(I32)
        chip_row = dev_row >> 1
        key = ((chip_row >> 2) * (1 + 3 * core) + (chip_row & 3) * (4 - 3 * core)) * 16 + lane_q
        key = jnp.where(n >= 0, key, -1)
        col = (dev_row & 1) * 128 + in_dev
        rows = lax.broadcasted_iota(I32, (256, T), 0)
        lhs[:, part * T : (part + 1) * T] = (rows == key).astype(F32).astype(BF16)
        rhs[:, part * T : (part + 1) * T] = (rows == col).astype(F32).astype(BF16)
    times = dot(lhs[...], rhs[...], NT).astype(BF16)
    csnd[:, 0] = times[:, 0:128].reshape(16, 16, 128)
    csnd[:, 1] = times[:, 128:256].reshape(16, 16, 128)
    crcv[me] = csnd[me]
    peers(lambda a_, b_, s: push(csnd.at[s], crcv.at[me], c_s.at[s], c_r.at[me], at(a_, b_)))
    lane = lax.broadcasted_iota(I32, (1, 64), 1)
    pos_row = jnp.full((1, 64), -1000, I32)
    for k in range(16):
        pos_row = jnp.where(lane == a * 16 + k, pos_ref[0, k], pos_row)
    pos_hot = (lax.broadcasted_iota(I32, (256, 64), 0) == pos_row + core * 128).astype(F32)
    own_lane = lax.broadcasted_iota(I32, (16, 64), 1) == a * 16 + lax.broadcasted_iota(I32, (16, 64), 0)

    def counts_ready():
        peers(lambda a_, b_, s: arrive(crcv.at[s], c_r.at[s], c_s.at[0]))
        for i in range(4):
            for k in range(2):
                ct[i, k * 128 : (k + 1) * 128, :] = (
                    crcv[i * 4 : i * 4 + 4, k].astype(F32).reshape(64, 128).T
                )
        ct[b] = ct[b] + pos_hot

    def scores(*blocks):
        def rows_of(h):
            got = [qown[pl.ds(b_ * 4, 4), h].reshape(64, H) for b_ in blocks]
            return got[0] if len(got) == 1 else jnp.concatenate(got, axis=0)

        s = dot(pb[:, 0:H], rows_of(0), NT)
        s = (s + dot(pb[:, H:D], rows_of(1), NT)) * HEAT
        return [s[:, i * 64 : (i + 1) * 64] for i in range(len(blocks))]

    def statistics(b_, s):
        c = ct[b_]
        named = c > 0.0
        top = jnp.max(jnp.where(named, s, -1e30), axis=0, keepdims=True)
        e = c * jnp.exp(jnp.where(named, s - top, -1e30))
        est[b_] = e
        stat[b_, 0:1, 0:64] = top
        stat[b_, 1:2, 0:64] = jnp.sum(e, axis=0, keepdims=True)
        stat[b_, 2:3, 0:64] = jnp.sum(e * s, axis=0, keepdims=True)

    got_full(slot(am, b))
    q_half(slot(am, b), 0, at(ap, b))
    q_full(slot(am, b), at(a, bp))
    q_full(slot(am, b), at(a, bm))
    got_full(slot(ap, b))
    q_half(slot(ap, b), 1, at(am, b))
    q_full(slot(ap, b), at(a, bp))
    q_full(slot(ap, b), at(a, bm))
    q_other(slot(am, b))
    q_other(slot(ap, b))
    got_full(slot(a, bm))
    q_half(slot(a, bm), 0, at(a, bp))
    got_full(slot(a, bp))
    q_half(slot(a, bp), 1, at(a, bm))
    got_halves(slot(a2, b))
    q_full(slot(a2, b), at(a, bp))
    q_full(slot(a2, b), at(a, bm))
    for a_ in (am, ap):
        got_full(slot(a_, bm))
        q_half(slot(a_, bm), 0, at(a, bp))
        got_full(slot(a_, bp))
        q_half(slot(a_, bp), 1, at(a, bm))
    q_other(slot(a2, b))
    for a_ in (a, am, ap):
        q_other(slot(a_, bm))
        q_other(slot(a_, bp))
    arrive(pb.at[other_rows], p_r, p_s)
    (s_b,) = scores(b)
    got_full(slot(a2, bm))
    q_half(slot(a2, bm), 0, at(a, bp))
    got_full(slot(a2, bp))
    q_half(slot(a2, bp), 1, at(a, bm))
    q_other(slot(a2, bm))
    q_other(slot(a2, bp))
    counts_ready()
    s_pos = jnp.sum(pos_hot * s_b, axis=0, keepdims=True)
    statistics(b, s_b)
    s_m, s_p = scores(bm, bp)
    statistics(bm, s_m)
    statistics(bp, s_p)
    for a_ in (a, am, ap, a2):
        got_halves(slot(a_, b2))
    (s_2,) = scores(b2)
    statistics(b2, s_2)
    peers(lambda a_, b_, s: push(stat, srcv.at[me], s_s.at[s], s_r.at[me], at(a_, b_)))
    srcv[me] = stat[...]
    for a_ in (a, am, ap, a2):
        q_other(slot(a_, b2))

    @pl.loop(1, 16)
    def _(k):
        zk = lax.rem(z + k, 16)
        cols = pl.ds(pl.multiple_of(zk * 256, 256), 256)
        arrive(ab.at[:, cols], ab_r.at[zk], ab_s.at[1])

    loads[6].wait()
    loads[7].wait()
    low_rows = dot(aq_ref[...], ab[0:16, :], NT).astype(BF16).astype(F32) * q_inv
    g_hi, g_lo = hi_lo(low_rows)
    gsnd[...] = jnp.zeros((16, 128), BF16)
    gsnd[:, 0:16] = g_hi
    gsnd[:, 16:32] = g_lo
    grcv[me] = gsnd[...]
    peers(lambda a_, b_, s: push(gsnd, grcv.at[me], g_s.at[s], g_r.at[me], at(a_, b_)))
    low_p = dot(ab[0:16, :], ap_ref[...], NT).astype(BF16)
    low_q = dot(ab[0:16, :], aq_ref[...], NT).astype(BF16)
    pbt = jnp.concatenate(hi_lo(dot(ab[16:32, :], pb[...], NT)), axis=0)
    block = pl.ds(b * 4, 4)
    ubt = dot(ab[16:32, 0:H], qown[block, 0].reshape(64, H), NT)
    ubt = ubt + dot(ab[16:32, H:D], qown[block, 1].reshape(64, H), NT)
    inv_row = jnp.sum(jnp.where(own_lane, q_inv, 0.0), axis=0, keepdims=True)

    peers(lambda a_, b_, s: arrive(srcv.at[s], s_r.at[s], s_s.at[0]))

    top = srcv[0, :, 0:1, :]
    for s in range(1, 16):
        top = jnp.maximum(top, srcv[s, :, 0:1, :])
    total = jnp.zeros((4, 1, 128), F32)
    first = jnp.zeros((4, 1, 128), F32)
    for s in range(16):
        f = jnp.exp(srcv[s, :, 0:1, :] - top)
        total = total + f * srcv[s, :, 1:2, :]
        first = first + f * srcv[s, :, 2:3, :]
    rows_s[:, 0:1, :] = jnp.exp(stat[:, 0:1, :] - top) * (HEAT / total)
    rows_s[:, 1:2, :] = first / total
    for i in range(4):
        est[i] = est[i] * rows_s[i, 0:1, 0:64]
    est[b] = est[b] - HEAT * pos_hot
    weight = jnp.concatenate([est[i] for i in range(4)], axis=1)
    w_hi, w_lo = hi_lo(weight)
    wt[0] = w_hi
    wt[1] = w_lo
    w_copy = push(wt.at[:, other_rows], woth, w_s, w_r, partner)
    inner_row = rows_s[b, 1:2, 0:64] - s_pos
    inner = lanes_sum(jnp.where(own_lane, inner_row, 0.0))

    for i in range(4):
        cols = slice(i * 64, (i + 1) * 64)
        share = dot(pbt, w_hi[:, cols]) + dot(pbt, w_lo[:, cols])
        ysnd[i, :, 0:64] = share[0:16] + share[16:32]
    peers(lambda a_, b_, s: push(ysnd.at[b_], yrcv.at[me], y_s.at[s], y_r.at[me], at(a_, b_)))
    yrcv[me] = ysnd[b]
    wq_hi, wq_lo = hi_lo(weight.T)
    wq[0] = wq_hi
    wq[1] = wq_lo

    def shares(b_, h, put):
        rows = pl.ds(pl.multiple_of(b_ * 64, 64), 64)
        w = jnp.concatenate([wq[0, rows, :], wq[1, rows, :]], axis=0)
        for j in range(H // T):
            r = dot(w, pb[:, h * H + j * T : h * H + (j + 1) * T])
            put(slice(j * T, (j + 1) * T), (r[0:64] + r[64:128]).reshape(4, 16, T))

    def put_in(ref, *where):
        def put(cols, r):
            ref[(*where, slice(None), slice(None), cols)] = r.astype(ref.dtype)

        return put

    rs = []

    def hop(src, dst, device):
        n = len(rs)
        rs.append(push(src, dst, rs_s.at[n], rs_r.at[n], device))

    def landed(dst, n):
        arrive(dst, rs_r.at[n], rs_s.at[0])

    shares(b2, 0, put_in(t1, 0))
    hop(t1.at[0], rl1.at[0], at(a, bp))
    shares(b2, 1, put_in(t1, 1))
    hop(t1.at[1], rl1.at[1], at(a, bm))
    shares(bp, 1, put_in(d1p, 1))
    hop(d1p.at[1], r1m.at[1], at(a, bp))
    shares(bm, 0, put_in(d1m, 0))
    hop(d1m.at[0], r1p.at[0], at(a, bm))

    for a_, b_ in ((am, b), (ap, b), (a2, b), (a, bm), (a, bp), (a, b)):
        arrive(qoth.at[slot(a_, b_)], qo_r.at[slot(a_, b_)], ag_s.at[0])
    for a_ in (am, ap, a2):
        for b_ in (bm, bp):
            arrive(qoth.at[slot(a_, b_)], qo_r.at[slot(a_, b_)], ag_s.at[0])
    for a_ in (a, am, ap, a2):
        arrive(qoth.at[slot(a_, b2)], qo_r.at[slot(a_, b2)], ag_s.at[0])
    arrive(woth, w_r, w_s)
    wa = jnp.concatenate([wt[0, own_rows, :], wt[1, own_rows, :]], axis=0)
    wb = jnp.concatenate([woth[0], woth[1]], axis=0)
    p_sq = jnp.zeros((128, 1), F32)
    p_in = jnp.zeros((128, 1), F32)
    for h in range(2):
        for j in range(H // T):
            cols = slice(h * H + j * T, h * H + (j + 1) * T)
            sub = slice(j * T, (j + 1) * T)
            r = dot(wa, qown[:, h, :, sub].reshape(256, T))
            r = r + dot(wb, qoth[:, h, :, sub].reshape(256, T))
            r = r[0:128] + r[128:256]
            pv = p_ref[:, cols].astype(F32)
            p_sq = p_sq + lanes_sum(pv * pv)
            p_in = p_in + lanes_sum(pv * r)
            pup[:, cols] = r
    p_inv = 1.0 / jnp.sqrt(p_sq + EPSILON)
    p_in = p_in * p_inv * p_inv
    for j in range(D // T):
        cols = slice(j * T, (j + 1) * T)
        gp_ref[:, cols] = ((pup[:, cols] - p_ref[:, cols].astype(F32) * p_in) * p_inv).astype(BF16)
    gp_out = pltpu.make_async_copy(gp_ref, gp_hbm, out_s.at[0])
    gp_out.start()

    back_p = dot(ab[16:32, :], gp_ref[...], NT).astype(BF16)
    peers(lambda a_, b_, s: arrive(grcv.at[s], g_r.at[s], g_s.at[0]))
    gall = grcv[...].reshape(256, 128)
    xt = (dot(wt[0], gall) + dot(wt[1], gall)).T
    xs = jnp.concatenate(hi_lo(xt[0:16] + xt[16:32]), axis=0)
    peers(lambda a_, b_, s: arrive(yrcv.at[s], y_r.at[s], y_s.at[0]))
    ysum = yrcv[0, :, 0:64]
    for s in range(1, 16):
        ysum = ysum + yrcv[s, :, 0:64]
    back = ((ysum - inner_row * ubt) * inv_row).astype(BF16)
    pick = lax.broadcasted_iota(I32, (64, 16), 0) == a * 16 + lax.broadcasted_iota(I32, (64, 16), 1)
    back_q = dot(back, pick.astype(F32).astype(BF16)).astype(BF16)
    for j in range(D // T):
        cols = slice(j * T, (j + 1) * T)
        r = dot(back_p, ap_ref[:, cols]) + dot(back_q, aq_ref[:, cols])
        dsum[0:16, cols] = ADAPTER_SCALE * r
        v2 = (q_ref[:, cols].astype(F32) * (inner * q_inv * q_inv)).astype(BF16)
        r = dot(xs, pb[:, cols])
        r = r[0:16] + r[16:32] + dot(low_p, gp_ref[:, cols]) - dot(low_q, v2)
        dsum[16:32, cols] = ADAPTER_SCALE * r
    mine = pl.ds(pl.multiple_of(core * 16, 16), 16)
    theirs = pl.ds(pl.multiple_of(other * 16, 16), 16)
    d_copy = push(dsum.at[theirs], dbuf, d_s, d_r, partner)

    shares(bp, 0, put_in(uf, 0))
    landed(rl1.at[0], 0)
    d1p[0] = (uf[0] + rl1[0].astype(F32)).astype(BF16)
    hop(d1p.at[0], r1m.at[0], at(a, bp))
    shares(bm, 1, put_in(uf, 1))
    landed(rl1.at[1], 1)
    d1m[1] = (uf[1] + rl1[1].astype(F32)).astype(BF16)
    hop(d1m.at[1], r1p.at[1], at(a, bm))

    arrive(dbuf, d_r, d_s)
    for j in range(D // 128):
        cols = slice(j * 128, (j + 1) * 128)
        drow[:, j // 2, j % 2, :] = dsum[mine, cols] + dbuf[:, cols]
    peers(lambda a_, b_, s: push(drow.at[s], rrow.at[me], rr_s.at[s], rr_r.at[me], at(a_, b_)))
    rrow[me] = drow[me]
    shares(b, 0, put_in(v1, 0))
    shares(b, 1, put_in(v1, 1))
    peers(lambda a_, b_, s: arrive(rrow.at[s], rr_r.at[s], rr_s.at[0]))
    acc = rrow[0]
    for s in range(1, 16):
        acc = acc + rrow[s]
    zrow[...] = acc

    @pl.loop(0, 15)
    def _(k):
        zk = lax.rem(z + lax.rem(k + 4, 15) + 1, 16)
        push(zrow.at[zk], zbuf.at[z], z_s.at[zk], z_r.at[z], (dp, zk))

    zbuf[z] = zrow[z]

    landed(r1m.at[1], 2)
    landed(r1p.at[0], 3)
    landed(r1m.at[0], 4)
    landed(r1p.at[1], 5)
    for h in range(2):
        v1[h] = v1[h] + r1m[h].astype(F32) + r1p[h].astype(F32)
        t2[h] = v1[h, a2].astype(BF16)
        if h == 0:
            hop(t2.at[0], rl2.at[0], at(ap, b))
            d2m[0] = v1[0, am].astype(BF16)
            hop(d2m.at[0], r2p.at[0], at(am, b))
        else:
            hop(t2.at[1], rl2.at[1], at(am, b))
            d2p[1] = v1[1, ap].astype(BF16)
            hop(d2p.at[1], r2m.at[1], at(ap, b))
    landed(rl2.at[0], 6)
    d2p[0] = (v1[0, ap] + rl2[0].astype(F32)).astype(BF16)
    hop(d2p.at[0], r2m.at[0], at(ap, b))
    landed(rl2.at[1], 8)
    d2m[1] = (v1[1, am] + rl2[1].astype(F32)).astype(BF16)
    hop(d2m.at[1], r2p.at[1], at(am, b))

    @pl.loop(1, 16)
    def _(k):
        zk = lax.rem(z + k, 16)
        arrive(zbuf.at[zk], z_r.at[zk], z_s.at[0])

    acc = zbuf[0]
    for s in range(1, 16):
        acc = acc + zbuf[s]
    orow[...] = acc
    oall[core, me] = acc

    @pl.loop(1, 32)
    def _(k):
        push(orow, oall.at[core, me], o_s.at[k], o_r.at[core, me], (lax.rem(dp + k, 32), z))

    landed(r2p.at[0], 7)
    landed(r2m.at[1], 9)
    landed(r2m.at[0], 10)
    landed(r2p.at[1], 11)
    qu = jnp.concatenate(
        [v1[h, a] + r2m[h].astype(F32) + r2p[h].astype(F32) for h in range(2)], axis=1
    )
    qv = q_ref[...].astype(F32)
    q_inv = 1.0 / jnp.sqrt(lanes_sum(qv * qv) + EPSILON)
    q_in = lanes_sum(qv * qu) * q_inv * q_inv
    gq_ref[...] = ((qu - qv * q_in) * q_inv).astype(BF16)
    gq_out = pltpu.make_async_copy(gq_ref, gq_hbm, out_s.at[1])
    gq_out.start()

    for c in sent + rs + [p_copy, d_copy, w_copy]:
        c.wait_send()

    @pl.loop(1, 16)
    def _(k):
        a_, b_ = near(a, lax.rem(k, 4)), near(b, k // 4)
        s = slot(a_, b_)
        gone(csnd.at[s], c_s.at[s], c_r.at[s])
        gone(stat, s_s.at[s], s_r.at[s])
        gone(gsnd, g_s.at[s], g_r.at[s])
        gone(ysnd.at[b_], y_s.at[s], y_r.at[s])
        gone(drow.at[s], rr_s.at[s], rr_r.at[s])
        zk = lax.rem(z + k, 16)
        gone(zrow.at[zk], z_s.at[zk], z_r.at[zk])
        gone(ab.at[:, zcols], ab_s.at[k], ab_r.at[z])

    @pl.loop(1, 32)
    def _(k):
        d_ = lax.rem(dp + k, 32)
        c_, h_ = lax.rem(d_, 2), d_ // 2
        s_ = (h_ // 4) * (1 + 3 * c_) + lax.rem(h_, 4) * (4 - 3 * c_)
        arrive(oall.at[c_, s_], o_r.at[c_, s_], o_s.at[1])

    outs = [gp_out, gq_out]
    for c_, dst in ((0, down_hbm), (1, up_hbm)):
        dv[c_, :, 0:128] = oall[c_, :, 0, :]
        dv[c_, :, 128:256] = oall[c_, :, 1, :]
        outs.append(pltpu.make_async_copy(dv.at[c_], dst, out_s.at[2 + c_]))
        outs[-1].start()

    @pl.loop(1, 32)
    def _(k):
        gone(orow, o_s.at[k], o_r.at[0, 0])

    for c in outs:
        c.wait()


ANY = pl.BlockSpec(memory_space=pl.ANY)
SM = pl.BlockSpec(memory_space=pltpu.SMEM)


def per_device(query, passage, query_attn, passage_attn, positives, negatives, home, down, up):
    dma = pltpu.SemaphoreType.DMA
    vm = pltpu.VMEM
    half = vm((2, 4, 16, H), BF16)
    row = vm((2, 16, H), BF16)
    grad_q, grad_p, sum_down, sum_up = pl.pallas_call(
        kernel,
        out_shape=(
            jax.ShapeDtypeStruct((16, D), BF16),
            jax.ShapeDtypeStruct((128, D), BF16),
            jax.ShapeDtypeStruct((16, 256), F32),
            jax.ShapeDtypeStruct((16, 256), F32),
        ),
        in_specs=[ANY] * 8 + [SM],
        out_specs=(ANY,) * 4,
        scratch_shapes=[
            vm((16, D), BF16),
            vm((128, D), BF16),
            vm((16, D), BF16),
            vm((128, D), BF16),
            vm((16, 64), I32),
            vm((32, 128), I32),
            vm((16, 256), BF16),
            vm((16, 256), BF16),
            vm((16, D), BF16),
            vm((128, D), BF16),
            vm((2, 16, 256), F32),
            vm((16, 2, 16, H), BF16),
            vm((16, 2, 16, H), BF16),
            vm((256, D), BF16),
            vm((32, D), BF16),
            vm((16, 128), I32),
            vm((256, H), BF16),
            vm((256, H), BF16),
            vm((16, 2, 16, 128), BF16),
            vm((16, 2, 16, 128), BF16),
            vm((4, 256, 64), F32),
            vm((4, 256, 64), F32),
            vm((4, 4, 128), F32),
            vm((16, 4, 4, 128), F32),
            vm((4, 4, 128), F32),
            vm((2, 256, 256), BF16),
            vm((2, 128, 256), BF16),
            vm((2, 256, 256), BF16),
            vm((16, 128), BF16),
            vm((16, 16, 128), BF16),
            vm((4, 16, 128), F32),
            vm((16, 16, 128), F32),
            half,
            half,
            half,
            half,
            half,
            half,
            vm((2, 4, 16, H), F32),
            vm((2, 4, 16, H), F32),
            row,
            row,
            row,
            row,
            row,
            row,
            vm((128, D), F32),
            vm((32, D), F32),
            vm((16, D), F32),
            vm((16, 16, 2, 128), F32),
            vm((16, 16, 2, 128), F32),
            vm((16, 2, 128), F32),
            vm((16, 2, 128), F32),
            vm((2, 128), F32),
            vm((2, 16, 2, 128), F32),
            dma((8,)),
            dma((4,)),
            dma((40,)),
            dma((16, 2)),
            dma((16,)),
            dma(()),
            dma(()),
            dma((16,)),
            dma((16,)),
            dma((16,)),
            dma((16,)),
            dma((16,)),
            dma((16,)),
            dma(()),
            dma(()),
            dma((16,)),
            dma((16,)),
            dma((16,)),
            dma((16,)),
            dma((12,)),
            dma((12,)),
            dma(()),
            dma(()),
            dma((16,)),
            dma((16,)),
            dma((16,)),
            dma((16,)),
            dma((32,)),
            dma((2, 16)),
        ],
        compiler_params=pltpu.CompilerParams(
            collective_id=0, has_side_effects=True, vmem_limit_bytes=60 * 1024 * 1024
        ),
    )(
        query[0], passage[0], query_attn[0], passage_attn[0], negatives[0],
        home[0].reshape(32, 128), down, up, positives,
    )
    return grad_q[None], grad_p[None], sum_down, sum_up


def solution(mesh):
    in_specs = (
        P("fsdp", "dp", None),
        P("fsdp", "dp", None),
        P("fsdp", "dp", None),
        P("fsdp", "dp", None),
        P("fsdp", "dp"),
        P("fsdp", "dp", None),
        P("fsdp", None),
        P(None, "fsdp"),
        P(None, "fsdp"),
    )
    out_specs = (P("fsdp", "dp", None), P("fsdp", "dp", None), P(None, "fsdp"), P(None, "fsdp"))
    return jax.shard_map(
        per_device, mesh=mesh, in_specs=in_specs, out_specs=out_specs, check_vma=False
    )
```

time: 101 us -> 81.4 us (0.81)
  Pallas kernels: 95.5 us -> 75.3 us
    pallas_call x1, Pallas kernels: 95.5 us -> 75.3 us  [per_device(): pl.pallas_call(kernel, out_shape=(jax.ShapeDtypeStruct((16, D), BF16), ja...]
    unnamed x4 -> x8, local copies, waits for them, and re-layouts: 2.95 us -> 5.2 us
where the time goes in v2:
time: 81.4 us; the launch traced here: 81.2 us
  Pallas kernels  75.3 us (93%)
  local copies, waits for them, and re-layouts  5.2 us (6%)
    pallas_call x1, Pallas kernels, per_device(): pl.pallas_call(kernel, out_shape=(jax.ShapeDtypeStruct((16, D), BF16), ja...  75.3 us
    unnamed x8, local copies, waits for them, and re-layouts  5.2 us

profile of v2, /device:TPU:1, one launch (start us, length us, event | category | flops | bytes accessed | tf_op | source)
XLA Modules:
  0.0 81.2 jit_solution(3093443223044696341)
XLA Ops:
  0.6 75.3 %shard_map.120 = (bf16[16,4096]{1,0:T(8,128)(2,1)}, bf16[128,4096]{1,0:T(8,128)(2,1)}, f32[16,256]{1,0:T(8,128)}, f32[16,256]{1,0:T(8,128)}) custom-call(bf16[16,4096]{1,0:T(8,128)(2,1)} %bitcast.12, bf16[128,4096]{1,0:T(8,128)(2,1)} %bitcast.9, bf16[16,4096]{1,0:T(8,128)(2,1)} %bitcast.13, bf16[128,4096]{1,0:T(8,128)(2,1)} %bitcast.10, s32[16,64]{1,0:T(8,128)} %bitcast.15, ...), custom_call_target="tpu_custom_call" | custom-call | tf_op jit(solution)/shard_map/pallas_call | solution.py:556
  76.0 1.6 %copy.17 = bf16[1,16,4096]{2,1,0:T(8,128)(2,1)} copy(bf16[1,16,4096]{2,1,0:T(8,128)(2,1)} %bitcast.11) | data formatting | bytes 262144
  77.6 0.0 copy-start.1
  77.6 2.3 %copy.18 = bf16[1,128,4096]{2,1,0:T(8,128)(2,1)} copy(bf16[1,128,4096]{2,1,0:T(8,128)(2,1)} %bitcast.8) | data formatting | bytes 2097152
  79.9 0.0 copy-done.1
  79.9 0.0 copy-start
  79.9 0.6 copy.19
  80.5 0.1 copy-done
  80.6 0.6 copy.20
Async XLA Ops:
  77.6 2.3 %copy-start.1 = (f32[16,256]{1,0:T(8,128)S(1)}, f32[16,256]{1,0:T(8,128)}, u32[]{:S(2)}) copy-start(f32[16,256]{1,0:T(8,128)} %get-tuple-element.18) | copy-start | bytes 49156
  79.9 0.7 copy-start

commit v3 on v2

v3 whole, which is shorter than its diff:
```python
import jax
import jax.numpy as jnp
from jax import lax
from jax.experimental import pallas as pl
from jax.experimental.pallas import tpu as pltpu
from jax.sharding import PartitionSpec as P

MESH = pl.DeviceIdType.MESH
F32, BF16, I32 = jnp.float32, jnp.bfloat16, jnp.int32
HEAT = 100.0
ADAPTER_SCALE = 2.0
EPSILON = 1e-06
D = 4096
H = 2048
T = 512
NN = (((1,), (0,)), ((), ()))
NT = (((1,), (1,)), ((), ()))


def dot(lhs, rhs, dims=NN):
    return lax.dot_general(lhs, rhs, dims, preferred_element_type=F32)


def hi_lo(w):
    hi = w.astype(BF16)
    return hi, (w - hi.astype(F32)).astype(BF16)


def lanes_sum(v):
    return jnp.sum(v, axis=-1, keepdims=True)


def kernel(
    q_hbm, p_hbm, aq_hbm, ap_hbm, neg_hbm, home_hbm, aw_hbm, bw_hbm, pos_hbm,
    gq_hbm, gp_hbm, down_hbm, up_hbm,
    q_ref, p_ref, aq_ref, ap_ref, neg_ref, home_ref, aw_ref, bw_ref, pos_ref, gq_ref, gp_ref, dv,
    qown, qoth, pb, ab, negp, lhs, rhs, csnd, crcv, ct, est, stat, srcv, rows_s,
    wt, woth, wq, gsnd, grcv, ysnd, yrcv,
    t1, rl1, d1p, d1m, r1m, r1p, uf, v1, t2, rl2, d2p, d2m, r2m, r2p,
    pinv, pup, dsum, dbuf, drow, rrow, zrow, zbuf, orow, oall,
    in_s, out_s, ag_s, q_r, qo_r, p_s, p_r, ab_s, ab_r, c_s, c_r, s_s, s_r, w_s, w_r, g_s, g_r, y_s, y_r,
    rs_s, rs_r, d_s, d_r, rr_s, rr_r, z_s, z_r, o_s, o_r,
):
    dp, z = lax.axis_index("dp"), lax.axis_index("fsdp")
    core, chip = lax.rem(dp, 2), dp // 2
    x, y = chip // 4, lax.rem(chip, 4)
    a = x * (1 - core) + y * core
    b = y * (1 - core) + x * core
    sa, sb = 8 - 6 * core, 2 + 6 * core
    other = 1 - core

    def near(v, k):
        return lax.rem(v + k, 4)

    def at(a_, b_):
        return (a_ * sa + b_ * sb + core, z)

    def slot(a_, b_):
        return b_ * 4 + a_

    me = slot(a, b)
    partner = (chip * 2 + other, z)
    am, a2, ap = near(a, 3), near(a, 2), near(a, 1)
    bm, b2, bp = near(b, 3), near(b, 2), near(b, 1)

    barrier = pltpu.get_barrier_semaphore()

    loads = [
        pltpu.make_async_copy(src, dst, in_s.at[i])
        for i, (src, dst) in enumerate(
            (
                (q_hbm, q_ref), (p_hbm, p_ref), (aw_hbm, aw_ref), (bw_hbm, bw_ref),
                (neg_hbm, neg_ref), (home_hbm, home_ref), (aq_hbm, aq_ref), (ap_hbm, ap_ref), (pos_hbm, pos_ref),
            )
        )
    ]
    loads[0].start()
    loads[1].start()

    @pl.loop(1, 32)
    def _(k):
        pl.semaphore_signal(barrier, inc=1, device_id=(lax.rem(dp + k, 32), z), device_id_type=MESH)

    @pl.loop(1, 16)
    def _(k):
        pl.semaphore_signal(barrier, inc=1, device_id=(dp, lax.rem(z + k, 16)), device_id_type=MESH)

    for c in loads[2:]:
        c.start()

    loads[0].wait()
    qv = q_ref[...].astype(F32)
    q_inv = 1.0 / jnp.sqrt(lanes_sum(qv * qv) + EPSILON)
    qe = (qv * q_inv).astype(BF16)
    qown[me, 0] = qe[:, :H]
    qown[me, 1] = qe[:, H:]
    for i in (2, 3):
        loads[i].wait()
    zcols = pl.ds(pl.multiple_of(z * 256, 256), 256)
    ab[0:16, zcols] = aw_ref[...]
    ab[16:32, zcols] = bw_ref[...]
    loads[1].wait()

    def p_rows(i, carry):
        rows = pl.ds(pl.multiple_of(i * 32, 32), 32)
        pv = p_ref[rows, :].astype(F32)
        inv = 1.0 / jnp.sqrt(lanes_sum(pv * pv) + EPSILON)
        pinv[rows, :] = jnp.broadcast_to(inv, (32, 128))
        dst = pl.ds(pl.multiple_of(core * 128 + i * 32, 32), 32)
        pb[dst, :] = (pv * inv).astype(BF16)
        return carry

    lax.fori_loop(0, 4, p_rows, 0)

    pl.semaphore_wait(barrier, 46)

    def push(src, dst, ssem, rsem, device):
        c = pltpu.make_async_remote_copy(
            src_ref=src, dst_ref=dst, send_sem=ssem, recv_sem=rsem, device_id=device, device_id_type=MESH
        )
        c.start()
        return c

    def arrive(dst, rsem, ssem):
        pltpu.make_async_remote_copy(
            src_ref=dst, dst_ref=dst, send_sem=ssem, recv_sem=rsem, device_id=partner, device_id_type=MESH
        ).wait_recv()

    def gone(src, ssem, rsem):
        pltpu.make_async_remote_copy(
            src_ref=src, dst_ref=src, send_sem=ssem, recv_sem=rsem, device_id=partner, device_id_type=MESH
        ).wait_send()

    def peers(body):
        def one(k):
            a_, b_ = near(a, lax.rem(6 - lax.rem(k, 4), 4)), near(b, lax.rem(6 - k // 4, 4))
            body(a_, b_, slot(a_, b_))

        pl.loop(0, 10)(one)
        pl.loop(11, 16)(one)

    def q_half(s, h, device):
        push(qown.at[s, h], qown.at[s, h], ag_s.at[0], q_r.at[s, h], device)

    def q_other(s):
        push(qown.at[s], qoth.at[s], ag_s.at[1], qo_r, partner)

    def got_half(s, h):
        arrive(qown.at[s, h], q_r.at[s, h], ag_s.at[0])

    q_half(me, 0, at(ap, b))
    q_half(me, 1, at(am, b))
    q_half(me, 1, at(ap, b))
    q_half(me, 0, at(am, b))
    own_rows = pl.ds(pl.multiple_of(core * 128, 128), 128)
    other_rows = pl.ds(pl.multiple_of(other * 128, 128), 128)
    p_copy = push(pb.at[own_rows], pb.at[own_rows], p_s, p_r, partner)
    q_other(me)

    @pl.loop(1, 16)
    def _(k):
        push(ab.at[:, zcols], ab.at[:, zcols], ab_s, ab_r, (dp, lax.rem(z + k, 16)))

    loads[4].wait()
    loads[5].wait()
    loads[8].wait()
    negp[...] = jnp.full((16, 128), -1, I32)
    negp[:, 0:64] = neg_ref[...]
    n_row = jnp.concatenate([negp[k : k + 1, :] for k in range(16)], axis=1)
    home = home_ref[...]
    table = jnp.concatenate(
        [(home >> 7).astype(F32).T, (home & 127).astype(F32).T], axis=0
    ).astype(BF16)
    for part in range(4):
        if part == 1:
            q_half(me, 0, at(a, bp))
            q_half(me, 1, at(a, bm))
            q_half(me, 1, at(a, bp))
            q_half(me, 0, at(a, bm))
        n = n_row[:, part * T : (part + 1) * T]
        lane_q = (lax.broadcasted_iota(I32, (1, T), 1) >> 7) + part * 4
        picked = (lax.broadcasted_iota(I32, (32, T), 0) == (n >> 7)).astype(F32).astype(BF16)
        found = dot(table, picked)
        low = lax.broadcasted_iota(I32, (128, T), 0) == (n & 127)
        dev_row = jnp.sum(jnp.where(low, found[0:128], 0.0), axis=0, keepdims=True).astype(I32)
        in_dev = jnp.sum(jnp.where(low, found[128:256], 0.0), axis=0, keepdims=True).astype(I32)
        chip_row = dev_row >> 1
        key = ((chip_row >> 2) * (1 + 3 * core) + (chip_row & 3) * (4 - 3 * core)) * 16 + lane_q
        key = jnp.where(n >= 0, key, -1)
        col = (dev_row & 1) * 128 + in_dev
        rows = lax.broadcasted_iota(I32, (256, T), 0)
        lhs[:, part * T : (part + 1) * T] = (rows == key).astype(F32).astype(BF16)
        rhs[:, part * T : (part + 1) * T] = (rows == col).astype(F32).astype(BF16)
    times = dot(lhs[...], rhs[...], NT).astype(BF16)
    csnd[:, 0] = times[:, 0:128].reshape(16, 16, 128)
    csnd[:, 1] = times[:, 128:256].reshape(16, 16, 128)
    crcv[me] = csnd[me]
    peers(lambda a_, b_, s: push(csnd.at[s], crcv.at[me], c_s, c_r, at(a_, b_)))
    lane = lax.broadcasted_iota(I32, (1, 64), 1)
    pos_row = jnp.full((1, 64), -1000, I32)
    for k in range(16):
        pos_row = jnp.where(lane == a * 16 + k, pos_ref[0, k], pos_row)
    pos_hot = (lax.broadcasted_iota(I32, (256, 64), 0) == pos_row + core * 128).astype(F32)
    own_lane = lax.broadcasted_iota(I32, (16, 64), 1) == a * 16 + lax.broadcasted_iota(I32, (16, 64), 0)

    def counts_ready():
        arrive(crcv.at[0:15], c_r, c_s)
        for i in range(4):
            for k in range(2):
                ct[i, k * 128 : (k + 1) * 128, :] = (
                    crcv[i * 4 : i * 4 + 4, k].astype(F32).reshape(64, 128).T
                )
        ct[b] = ct[b] + pos_hot

    def scores(*blocks):
        def rows_of(h):
            got = [qown[pl.ds(b_ * 4, 4), h].reshape(64, H) for b_ in blocks]
            return got[0] if len(got) == 1 else jnp.concatenate(got, axis=0)

        s = dot(pb[:, 0:H], rows_of(0), NT)
        s = (s + dot(pb[:, H:D], rows_of(1), NT)) * HEAT
        return [s[:, i * 64 : (i + 1) * 64] for i in range(len(blocks))]

    def statistics(b_, s):
        c = ct[b_]
        named = c > 0.0
        top = jnp.max(jnp.where(named, s, -1e30), axis=0, keepdims=True)
        e = c * jnp.exp(jnp.where(named, s - top, -1e30))
        est[b_] = e
        stat[b_, 0:1, 0:64] = top
        stat[b_, 1:2, 0:64] = jnp.sum(e, axis=0, keepdims=True)
        stat[b_, 2:3, 0:64] = jnp.sum(e * s, axis=0, keepdims=True)

    got_half(slot(am, b), 0)
    q_half(slot(am, b), 0, at(ap, b))
    q_half(slot(am, b), 0, at(a, bp))
    got_half(slot(ap, b), 1)
    q_half(slot(ap, b), 1, at(am, b))
    q_half(slot(ap, b), 1, at(a, bm))
    got_half(slot(am, b), 1)
    q_half(slot(am, b), 1, at(a, bm))
    q_half(slot(am, b), 1, at(a, bp))
    got_half(slot(ap, b), 0)
    q_half(slot(ap, b), 0, at(a, bp))
    q_half(slot(ap, b), 0, at(a, bm))
    q_half(slot(am, b), 0, at(a, bm))
    q_half(slot(ap, b), 1, at(a, bp))
    q_other(slot(am, b))
    q_other(slot(ap, b))
    got_half(slot(a, bm), 0)
    q_half(slot(a, bm), 0, at(a, bp))
    got_half(slot(a, bp), 1)
    q_half(slot(a, bp), 1, at(a, bm))
    got_half(slot(a2, b), 0)
    q_half(slot(a2, b), 0, at(a, bp))
    got_half(slot(a2, b), 1)
    q_half(slot(a2, b), 1, at(a, bm))
    q_half(slot(a2, b), 1, at(a, bp))
    q_half(slot(a2, b), 0, at(a, bm))
    q_other(slot(a2, b))
    arrive(pb.at[other_rows], p_r, p_s)
    (s_b,) = scores(b)
    for a_ in (am, ap):
        got_half(slot(a_, bm), 0)
        q_half(slot(a_, bm), 0, at(a, bp))
        got_half(slot(a_, bp), 1)
        q_half(slot(a_, bp), 1, at(a, bm))
    counts_ready()
    s_pos = jnp.sum(pos_hot * s_b, axis=0, keepdims=True)
    statistics(b, s_b)
    got_half(slot(a2, bm), 0)
    q_half(slot(a2, bm), 0, at(a, bp))
    got_half(slot(a2, bp), 1)
    q_half(slot(a2, bp), 1, at(a, bm))
    for a_ in (a, am, ap, a2):
        got_half(slot(a_, bm), 1)
        got_half(slot(a_, bp), 0)
        q_other(slot(a_, bm))
        q_other(slot(a_, bp))
    s_m, s_p = scores(bm, bp)
    statistics(bm, s_m)
    statistics(bp, s_p)
    for a_ in (a, am, ap, a2):
        for h in range(2):
            got_half(slot(a_, b2), h)
    (s_2,) = scores(b2)
    statistics(b2, s_2)
    peers(lambda a_, b_, s: push(stat, srcv.at[me], s_s, s_r, at(a_, b_)))
    srcv[me] = stat[...]
    for a_ in (a, am, ap, a2):
        q_other(slot(a_, b2))

    arrive(ab.at[:, 0 : 15 * 256], ab_r, ab_s)
    loads[6].wait()
    loads[7].wait()
    low_rows = dot(aq_ref[...], ab[0:16, :], NT).astype(BF16).astype(F32) * q_inv
    g_hi, g_lo = hi_lo(low_rows)
    gsnd[...] = jnp.zeros((16, 128), BF16)
    gsnd[:, 0:16] = g_hi
    gsnd[:, 16:32] = g_lo
    grcv[me] = gsnd[...]
    peers(lambda a_, b_, s: push(gsnd, grcv.at[me], g_s, g_r, at(a_, b_)))
    low_p = dot(ab[0:16, :], ap_ref[...], NT).astype(BF16)
    low_q = dot(ab[0:16, :], aq_ref[...], NT).astype(BF16)
    pbt = jnp.concatenate(hi_lo(dot(ab[16:32, :], pb[...], NT)), axis=0)
    block = pl.ds(b * 4, 4)
    ubt = dot(ab[16:32, 0:H], qown[block, 0].reshape(64, H), NT)
    ubt = ubt + dot(ab[16:32, H:D], qown[block, 1].reshape(64, H), NT)
    inv_row = jnp.sum(jnp.where(own_lane, q_inv, 0.0), axis=0, keepdims=True)

    arrive(srcv.at[0:15], s_r, s_s)

    top = srcv[0, :, 0:1, :]
    for s in range(1, 16):
        top = jnp.maximum(top, srcv[s, :, 0:1, :])
    total = jnp.zeros((4, 1, 128), F32)
    first = jnp.zeros((4, 1, 128), F32)
    for s in range(16):
        f = jnp.exp(srcv[s, :, 0:1, :] - top)
        total = total + f * srcv[s, :, 1:2, :]
        first = first + f * srcv[s, :, 2:3, :]
    rows_s[:, 0:1, :] = jnp.exp(stat[:, 0:1, :] - top) * (HEAT / total)
    rows_s[:, 1:2, :] = first / total
    for i in range(4):
        est[i] = est[i] * rows_s[i, 0:1, 0:64]
    est[b] = est[b] - HEAT * pos_hot
    weight = jnp.concatenate([est[i] for i in range(4)], axis=1)
    w_hi, w_lo = hi_lo(weight)
    wt[0] = w_hi
    wt[1] = w_lo
    w_copy = push(wt.at[:, other_rows], woth, w_s, w_r, partner)
    inner_row = rows_s[b, 1:2, 0:64] - s_pos
    inner = lanes_sum(jnp.where(own_lane, inner_row, 0.0))

    for i in range(4):
        cols = slice(i * 64, (i + 1) * 64)
        share = dot(pbt, w_hi[:, cols]) + dot(pbt, w_lo[:, cols])
        ysnd[i, :, 0:64] = share[0:16] + share[16:32]
    peers(lambda a_, b_, s: push(ysnd.at[b_], yrcv.at[me], y_s, y_r, at(a_, b_)))
    yrcv[me] = ysnd[b]
    arrive(grcv.at[0:15], g_r, g_s)
    gall = grcv[...].reshape(256, 128)
    xt = (dot(wt[0], gall) + dot(wt[1], gall)).T
    xs = jnp.concatenate(hi_lo(xt[0:16] + xt[16:32]), axis=0)

    wq_hi, wq_lo = hi_lo(weight.T)
    wq[0] = wq_hi
    wq[1] = wq_lo

    def shares(b_, h, put):
        rows = pl.ds(pl.multiple_of(b_ * 64, 64), 64)
        w = jnp.concatenate([wq[0, rows, :], wq[1, rows, :]], axis=0)
        for j in range(H // T):
            r = dot(w, pb[:, h * H + j * T : h * H + (j + 1) * T])
            put(slice(j * T, (j + 1) * T), (r[0:64] + r[64:128]).reshape(4, 16, T))

    def put_in(ref, *where):
        def put(cols, r):
            ref[(*where, slice(None), slice(None), cols)] = r.astype(ref.dtype)

        return put

    rs = []

    def hop(n, src, dst, device):
        rs.append(push(src, dst, rs_s.at[n], rs_r.at[n], device))

    def landed(dst, n):
        arrive(dst, rs_r.at[n], rs_s.at[0])

    shares(b2, 0, put_in(t1, 0))
    hop(0, t1.at[0], rl1.at[0], at(a, bp))
    shares(b2, 1, put_in(t1, 1))
    hop(1, t1.at[1], rl1.at[1], at(a, bm))

    def two_parts(w, q, h, sub):
        r = dot(w, q[:, h, :, sub].reshape(256, T))
        return r[0:128] + r[128:256]

    wa = jnp.concatenate([wt[0, own_rows, :], wt[1, own_rows, :]], axis=0)
    for h in range(2):
        for j in range(H // T):
            cols = slice(h * H + j * T, h * H + (j + 1) * T)
            pup[:, cols] = two_parts(wa, qown, h, slice(j * T, (j + 1) * T))
            r = dot(xs, pb[:, cols])
            dsum[16:32, cols] = r[0:16] + r[16:32]
    arrive(qoth, qo_r, ag_s.at[1])
    arrive(woth, w_r, w_s)
    wb = jnp.concatenate([woth[0], woth[1]], axis=0)
    p_in = jnp.zeros((128, 1), F32)
    for h in range(2):
        for j in range(H // T):
            cols = slice(h * H + j * T, h * H + (j + 1) * T)
            r = pup[:, cols] + two_parts(wb, qoth, h, slice(j * T, (j + 1) * T))
            p_in = p_in + lanes_sum(p_ref[:, cols].astype(F32) * r)
            pup[:, cols] = r
    p_inv = pinv[:, 0:1]
    p_in = p_in * p_inv * p_inv
    for j in range(D // T):
        cols = slice(j * T, (j + 1) * T)
        gp_ref[:, cols] = ((pup[:, cols] - p_ref[:, cols].astype(F32) * p_in) * p_inv).astype(BF16)
    gp_out = pltpu.make_async_copy(gp_ref, gp_hbm, out_s.at[0])
    gp_out.start()

    back_p = dot(ab[16:32, :], gp_ref[...], NT).astype(BF16)
    arrive(yrcv.at[0:15], y_r, y_s)
    ysum = yrcv[0, :, 0:64]
    for s in range(1, 16):
        ysum = ysum + yrcv[s, :, 0:64]
    back = ((ysum - inner_row * ubt) * inv_row).astype(BF16)
    pick = lax.broadcasted_iota(I32, (64, 16), 0) == a * 16 + lax.broadcasted_iota(I32, (64, 16), 1)
    back_q = dot(back, pick.astype(F32).astype(BF16)).astype(BF16)
    back_all = jnp.concatenate([back_p, back_q], axis=1)
    low_all = jnp.concatenate([low_p, -low_q], axis=1)
    for j in range(D // T):
        cols = slice(j * T, (j + 1) * T)
        r = dot(back_all, jnp.concatenate([ap_ref[:, cols], aq_ref[:, cols]], axis=0))
        dsum[0:16, cols] = ADAPTER_SCALE * r
        v2 = (q_ref[:, cols].astype(F32) * (inner * q_inv * q_inv)).astype(BF16)
        r = dot(low_all, jnp.concatenate([gp_ref[:, cols], v2], axis=0))
        dsum[16:32, cols] = ADAPTER_SCALE * (dsum[16:32, cols] + r)
    mine = pl.ds(pl.multiple_of(core * 16, 16), 16)
    theirs = pl.ds(pl.multiple_of(other * 16, 16), 16)
    d_copy = push(dsum.at[theirs], dbuf, d_s, d_r, partner)

    shares(bp, 1, put_in(d1p, 1))
    shares(bm, 0, put_in(d1m, 0))
    shares(bp, 0, put_in(uf, 0))
    shares(bm, 1, put_in(uf, 1))

    arrive(dbuf, d_r, d_s)
    for j in range(D // 128):
        cols = slice(j * 128, (j + 1) * 128)
        drow[:, j // 2, j % 2, :] = dsum[mine, cols] + dbuf[:, cols]
    peers(lambda a_, b_, s: push(drow.at[s], rrow.at[me], rr_s, rr_r, at(a_, b_)))
    rrow[me] = drow[me]
    hop(2, d1p.at[1], r1m.at[1], at(a, bp))
    hop(3, d1m.at[0], r1p.at[0], at(a, bm))
    landed(rl1.at[0], 0)
    d1p[0] = (uf[0] + rl1[0].astype(F32)).astype(BF16)
    hop(4, d1p.at[0], r1m.at[0], at(a, bp))
    landed(rl1.at[1], 1)
    d1m[1] = (uf[1] + rl1[1].astype(F32)).astype(BF16)
    hop(5, d1m.at[1], r1p.at[1], at(a, bm))
    shares(b, 0, put_in(v1, 0))
    shares(b, 1, put_in(v1, 1))
    arrive(rrow.at[0:15], rr_r, rr_s)
    acc = rrow[0]
    for s in range(1, 16):
        acc = acc + rrow[s]
    zrow[...] = acc

    @pl.loop(0, 15)
    def _(k):
        zk = lax.rem(z + lax.rem(k + 4, 15) + 1, 16)
        push(zrow.at[zk], zbuf.at[z], z_s, z_r, (dp, zk))

    zbuf[z] = zrow[z]

    landed(r1m.at[1], 2)
    landed(r1p.at[0], 3)
    landed(r1m.at[0], 4)
    landed(r1p.at[1], 5)
    for h in range(2):
        v1[h] = v1[h] + r1m[h].astype(F32) + r1p[h].astype(F32)
        t2[h] = v1[h, a2].astype(BF16)
        if h == 0:
            hop(6, t2.at[0], rl2.at[0], at(ap, b))
            d2m[0] = v1[0, am].astype(BF16)
            hop(7, d2m.at[0], r2p.at[0], at(am, b))
        else:
            hop(8, t2.at[1], rl2.at[1], at(am, b))
            d2p[1] = v1[1, ap].astype(BF16)
            hop(9, d2p.at[1], r2m.at[1], at(ap, b))
    arrive(zbuf.at[0:15], z_r, z_s)
    acc = zbuf[0]
    for s in range(1, 16):
        acc = acc + zbuf[s]
    orow[...] = acc
    oall[core * 16 + me] = acc

    @pl.loop(1, 32)
    def _(k):
        push(orow, oall.at[core * 16 + me], o_s, o_r, (lax.rem(dp + k, 32), z))

    landed(rl2.at[0], 6)
    d2p[0] = (v1[0, ap] + rl2[0].astype(F32)).astype(BF16)
    hop(10, d2p.at[0], r2m.at[0], at(ap, b))
    landed(rl2.at[1], 8)
    d2m[1] = (v1[1, am] + rl2[1].astype(F32)).astype(BF16)
    hop(11, d2m.at[1], r2p.at[1], at(am, b))
    landed(r2p.at[0], 7)
    landed(r2m.at[1], 9)
    landed(r2m.at[0], 10)
    landed(r2p.at[1], 11)
    qu = jnp.concatenate(
        [v1[h, a] + r2m[h].astype(F32) + r2p[h].astype(F32) for h in range(2)], axis=1
    )
    qv = q_ref[...].astype(F32)
    q_inv = 1.0 / jnp.sqrt(lanes_sum(qv * qv) + EPSILON)
    q_in = lanes_sum(qv * qu) * q_inv * q_inv
    gq_ref[...] = ((qu - qv * q_in) * q_inv).astype(BF16)
    gq_out = pltpu.make_async_copy(gq_ref, gq_hbm, out_s.at[1])
    gq_out.start()

    for c in rs + [p_copy, d_copy, w_copy]:
        c.wait_send()
    gone(qown.at[0:15], ag_s.at[0], q_r.at[0, 0])
    gone(qown, ag_s.at[1], qo_r)
    gone(ab.at[:, 0 : 15 * 256], ab_s, ab_r)
    gone(csnd.at[0:15], c_s, c_r)
    gone(srcv.at[0:15], s_s, s_r)
    gone(grcv.at[0:15], g_s, g_r)
    gone(yrcv.at[0:15], y_s, y_r)
    gone(drow.at[0:15], rr_s, rr_r)
    gone(zrow.at[0:15], z_s, z_r)
    gone(oall.at[0:31], o_s, o_r)
    arrive(oall.at[0:31], o_r, o_s)
    outs = [gp_out, gq_out]
    for c_, dst in ((0, down_hbm), (1, up_hbm)):
        dv[c_, :, 0:128] = oall[c_ * 16 : c_ * 16 + 16, 0, :]
        dv[c_, :, 128:256] = oall[c_ * 16 : c_ * 16 + 16, 1, :]
        outs.append(pltpu.make_async_copy(dv.at[c_], dst, out_s.at[2 + c_]))
        outs[-1].start()

    for c in outs:
        c.wait()


def hand_over(*refs):
    copies = [pltpu.make_async_copy(refs[i], refs[4 + i], refs[8].at[i]) for i in (1, 0, 2, 3)]
    for c in copies:
        c.start()
    for c in copies:
        c.wait()


ANY = pl.BlockSpec(memory_space=pl.ANY)


def per_device(query, passage, query_attn, passage_attn, positives, negatives, home, down, up):
    dma = pltpu.SemaphoreType.DMA
    vm = pltpu.VMEM
    half = vm((2, 4, 16, H), BF16)
    row = vm((2, 16, H), BF16)
    grad_q, grad_p, sum_down, sum_up = pl.pallas_call(
        kernel,
        out_shape=(
            jax.ShapeDtypeStruct((16, D), BF16),
            jax.ShapeDtypeStruct((128, D), BF16),
            jax.ShapeDtypeStruct((16, 256), F32),
            jax.ShapeDtypeStruct((16, 256), F32),
        ),
        in_specs=[pl.BlockSpec(memory_space=pltpu.HBM)] * 9,
        out_specs=(ANY,) * 4,
        scratch_shapes=[
            vm((16, D), BF16),
            vm((128, D), BF16),
            vm((16, D), BF16),
            vm((128, D), BF16),
            vm((16, 64), I32),
            vm((32, 128), I32),
            vm((16, 256), BF16),
            vm((16, 256), BF16),
            pltpu.SMEM((1, 16), I32),
            vm((16, D), BF16),
            vm((128, D), BF16),
            vm((2, 16, 256), F32),
            vm((16, 2, 16, H), BF16),
            vm((16, 2, 16, H), BF16),
            vm((256, D), BF16),
            vm((32, D), BF16),
            vm((16, 128), I32),
            vm((256, H), BF16),
            vm((256, H), BF16),
            vm((16, 2, 16, 128), BF16),
            vm((16, 2, 16, 128), BF16),
            vm((4, 256, 64), F32),
            vm((4, 256, 64), F32),
            vm((4, 4, 128), F32),
            vm((16, 4, 4, 128), F32),
            vm((4, 4, 128), F32),
            vm((2, 256, 256), BF16),
            vm((2, 128, 256), BF16),
            vm((2, 256, 256), BF16),
            vm((16, 128), BF16),
            vm((16, 16, 128), BF16),
            vm((4, 16, 128), F32),
            vm((16, 16, 128), F32),
            half,
            half,
            half,
            half,
            half,
            half,
            vm((2, 4, 16, H), F32),
            vm((2, 4, 16, H), F32),
            row,
            row,
            row,
            row,
            row,
            row,
            vm((128, 128), F32),
            vm((128, D), F32),
            vm((32, D), F32),
            vm((16, D), F32),
            vm((16, 16, 2, 128), F32),
            vm((16, 16, 2, 128), F32),
            vm((16, 2, 128), F32),
            vm((16, 2, 128), F32),
            vm((2, 128), F32),
            vm((32, 2, 128), F32),
            dma((9,)),
            dma((4,)),
            dma((2,)),
            dma((16, 2)),
            dma(()),
            dma(()),
            dma(()),
            dma(()),
            dma(()),
            dma(()),
            dma(()),
            dma(()),
            dma(()),
            dma(()),
            dma(()),
            dma(()),
            dma(()),
            dma(()),
            dma(()),
            dma((12,)),
            dma((12,)),
            dma(()),
            dma(()),
            dma(()),
            dma(()),
            dma(()),
            dma(()),
            dma(()),
            dma(()),
        ],
        compiler_params=pltpu.CompilerParams(
            collective_id=0, has_side_effects=True, vmem_limit_bytes=26 * 1024 * 1024
        ),
    )(
        *(
            pltpu.with_memory_space_constraint(v, pltpu.HBM)
            for v in (
                query[0], passage[0], query_attn[0], passage_attn[0], negatives[0],
                home[0].reshape(32, 128), down, up, positives,
            )
        )
    )
    outs = pl.pallas_call(
        hand_over,
        out_shape=tuple(jax.ShapeDtypeStruct(v.shape, v.dtype) for v in (grad_q, grad_p, sum_down, sum_up)),
        in_specs=[ANY] * 4,
        out_specs=(ANY,) * 4,
        scratch_shapes=[dma((4,))],
        compiler_params=pltpu.CompilerParams(vmem_limit_bytes=1024 * 1024),
    )(grad_q, grad_p, sum_down, sum_up)
    return outs[0][None], outs[1][None], outs[2], outs[3]


def solution(mesh):
    in_specs = (
        P("fsdp", "dp", None),
        P("fsdp", "dp", None),
        P("fsdp", "dp", None),
        P("fsdp", "dp", None),
        P("fsdp", "dp"),
        P("fsdp", "dp", None),
        P("fsdp", None),
        P(None, "fsdp"),
        P(None, "fsdp"),
    )
    out_specs = (P("fsdp", "dp", None), P("fsdp", "dp", None), P(None, "fsdp"), P(None, "fsdp"))
    return jax.shard_map(
        per_device, mesh=mesh, in_specs=in_specs, out_specs=out_specs, check_vma=False
    )
```

time: 81.4 us -> 69.6 us (0.86)
  Pallas kernels: 75.3 us -> 68.4 us
  local copies, waits for them, and re-layouts: 5.2 us -> 0 us
    pallas_call x1, Pallas kernels: 75.3 us -> 67.4 us  [per_device(): pl.pallas_call(kernel, out_shape=(jax.ShapeDtypeStruct((16, D), BF16), ja...]
    unnamed x8 -> x0, local copies, waits for them, and re-layouts: 5.2 us -> none
    pallas_call x0 -> x1, Pallas kernels: none -> 1.04 us  [per_device(): pl.pallas_call(hand_over, out_shape=tuple((jax.ShapeDtypeStruct(v.shape,...]
where the time goes in v3:
time: 69.6 us; the launch traced here: 69 us
  Pallas kernels  68.4 us (98%)
    pallas_call x1, Pallas kernels, per_device(): pl.pallas_call(kernel, out_shape=(jax.ShapeDtypeStruct((16, D), BF16), ja...  67.4 us

profile of v3, /device:TPU:1, one launch (start us, length us, event | category | flops | bytes accessed | tf_op | source)
XLA Modules:
  0.0 69.0 jit_solution(10548266526758172621)
XLA Ops:
  0.6 67.4 %shard_map.120 = (bf16[16,4096]{1,0:T(8,128)(2,1)S(1)}, bf16[128,4096]{1,0:T(8,128)(2,1)S(1)}, f32[16,256]{1,0:T(8,128)S(1)}, f32[16,256]{1,0:T(8,128)S(1)}) custom-call(bf16[16,4096]{1,0:T(8,128)(2,1)} %bitcast.10, bf16[128,4096]{1,0:T(8,128)(2,1)} %bitcast.8, bf16[16,4096]{1,0:T(8,128)(2,1)} %bitcast.11, bf16[128,4096]{1,0:T(8,128)(2,1)} %bitcast.9, ...), custom_call_target="tpu_custom_call" | custom-call | tf_op jit(solution)/shard_map/pallas_call | solution.py:546
  68.0 1.0 %shard_map.121 = (bf16[16,4096]{1,0:T(8,128)(2,1)}, bf16[128,4096]{1,0:T(8,128)(2,1)}, f32[16,256]{1,0:T(8,128)}, f32[16,256]{1,0:T(8,128)}) custom-call(bf16[16,4096]{1,0:T(8,128)(2,1)S(1)} %get-tuple-element.12.refs_0_, bf16[128,4096]{1,0:T(8,128)(2,1)S(1)} %get-tuple-element.13.refs_1_, f32[16,256]{1,0:T(8,128)S(1)} %get-tuple-element.14.refs_2_, ...), custom_call_target="tpu_custom_call" | custom-call | tf_op jit(solution)/shard_map/pallas_call | solution.py:656

commit v4 on v3

--- a/solution.py
+++ b/solution.py
@@ -38,7 +38,7 @@
     wt, woth, wq, gsnd, grcv, ysnd, yrcv,
     t1, rl1, d1p, d1m, r1m, r1p, uf, v1, t2, rl2, d2p, d2m, r2m, r2p,
     pinv, pup, dsum, dbuf, drow, rrow, zrow, zbuf, orow, oall,
-    in_s, out_s, ag_s, q_r, qo_r, p_s, p_r, ab_s, ab_r, c_s, c_r, s_s, s_r, w_s, w_r, g_s, g_r, y_s, y_r,
+    in_s, out_s, ag_s, q_r, qo_r, p_s, p_r, ab_s, ab_r, abp_s, abp_r, near_s, c_s, c_r, s_s, s_r, w_s, w_r, g_s, g_r, y_s, y_r,
     rs_s, rs_r, d_s, d_r, rr_s, rr_r, z_s, z_r, o_s, o_r,
 ):
     dp, z = lax.axis_index("dp"), lax.axis_index("fsdp")
@@ -77,13 +77,18 @@
     loads[0].start()
     loads[1].start()
 
-    @pl.loop(1, 32)
-    def _(k):
-        pl.semaphore_signal(barrier, inc=1, device_id=(lax.rem(dp + k, 32), z), device_id_type=MESH)
-
-    @pl.loop(1, 16)
-    def _(k):
-        pl.semaphore_signal(barrier, inc=1, device_id=(dp, lax.rem(z + k, 16)), device_id_type=MESH)
+    def tell_plane(sem):
+        for device in (at(ap, b), at(am, b), at(a, bp), at(a, bm)):
+            pl.semaphore_signal(sem, inc=1, device_id=device, device_id_type=MESH)
+
+    pl.semaphore_signal(barrier, inc=1, device_id=partner, device_id_type=MESH)
+    tell_plane(barrier)
+
+    def tell_z(sem, step):
+        for k in (step, 16 - step):
+            pl.semaphore_signal(sem, inc=1, device_id=(dp, lax.rem(z + k, 16)), device_id_type=MESH)
+
+    tell_z(barrier, 1)
 
     for c in loads[2:]:
         c.start()
@@ -97,8 +102,9 @@
     for i in (2, 3):
         loads[i].wait()
     zcols = pl.ds(pl.multiple_of(z * 256, 256), 256)
-    ab[0:16, zcols] = aw_ref[...]
-    ab[16:32, zcols] = bw_ref[...]
+    kind = pl.ds(pl.multiple_of(core * 16, 16), 16)
+    other_kind = pl.ds(pl.multiple_of(other * 16, 16), 16)
+    ab[kind, zcols] = jnp.where(core == 0, aw_ref[...], bw_ref[...])
     loads[1].wait()
 
     def p_rows(i, carry):
@@ -112,7 +118,9 @@
 
     lax.fori_loop(0, 4, p_rows, 0)
 
-    pl.semaphore_wait(barrier, 46)
+    pl.semaphore_wait(barrier, 7)
+    tell_z(near_s.at[0], 1)
+    tell_plane(near_s.at[3])
 
     def push(src, dst, ssem, rsem, device):
         c = pltpu.make_async_remote_copy(
@@ -156,10 +164,6 @@
     other_rows = pl.ds(pl.multiple_of(other * 128, 128), 128)
     p_copy = push(pb.at[own_rows], pb.at[own_rows], p_s, p_r, partner)
     q_other(me)
-
-    @pl.loop(1, 16)
-    def _(k):
-        push(ab.at[:, zcols], ab.at[:, zcols], ab_s, ab_r, (dp, lax.rem(z + k, 16)))
 
     loads[4].wait()
     loads[5].wait()
@@ -195,7 +199,6 @@
     csnd[:, 0] = times[:, 0:128].reshape(16, 16, 128)
     csnd[:, 1] = times[:, 128:256].reshape(16, 16, 128)
     crcv[me] = csnd[me]
-    peers(lambda a_, b_, s: push(csnd.at[s], crcv.at[me], c_s, c_r, at(a_, b_)))
     lane = lax.broadcasted_iota(I32, (1, 64), 1)
     pos_row = jnp.full((1, 64), -1000, I32)
     for k in range(16):
@@ -227,16 +230,24 @@
         top = jnp.max(jnp.where(named, s, -1e30), axis=0, keepdims=True)
         e = c * jnp.exp(jnp.where(named, s - top, -1e30))
         est[b_] = e
-        stat[b_, 0:1, 0:64] = top
-        stat[b_, 1:2, 0:64] = jnp.sum(e, axis=0, keepdims=True)
-        stat[b_, 2:3, 0:64] = jnp.sum(e * s, axis=0, keepdims=True)
-
+        side = (lax.broadcasted_iota(I32, (1, 128), 1) >> 6) == lax.rem(b_, 2)
+        sums = (top, jnp.sum(e, axis=0, keepdims=True), jnp.sum(e * s, axis=0, keepdims=True))
+        for k, v in enumerate(sums):
+            row = stat[b_ // 2, k : k + 1, :]
+            stat[b_ // 2, k : k + 1, :] = jnp.where(side, jnp.concatenate([v, v], axis=1), row)
+
+    pl.semaphore_wait(near_s.at[0], 2)
+    tell_z(near_s.at[1], 2)
+    pl.semaphore_wait(near_s.at[3], 4)
+    tell_plane(near_s.at[4])
     got_half(slot(am, b), 0)
     q_half(slot(am, b), 0, at(ap, b))
     q_half(slot(am, b), 0, at(a, bp))
     got_half(slot(ap, b), 1)
     q_half(slot(ap, b), 1, at(am, b))
     q_half(slot(ap, b), 1, at(a, bm))
+    pl.semaphore_wait(near_s.at[4], 4)
+    tell_plane(near_s.at[5])
     got_half(slot(am, b), 1)
     q_half(slot(am, b), 1, at(a, bm))
     q_half(slot(am, b), 1, at(a, bp))
@@ -247,10 +258,10 @@
     q_half(slot(ap, b), 1, at(a, bp))
     q_other(slot(am, b))
     q_other(slot(ap, b))
-    got_half(slot(a, bm), 0)
-    q_half(slot(a, bm), 0, at(a, bp))
-    got_half(slot(a, bp), 1)
-    q_half(slot(a, bp), 1, at(a, bm))
+    pl.semaphore_wait(near_s.at[1], 2)
+    tell_z(near_s.at[2], 4)
+    pl.semaphore_wait(near_s.at[5], 4)
+    peers(lambda a_, b_, s: push(csnd.at[s], crcv.at[me], c_s, c_r, at(a_, b_)))
     got_half(slot(a2, b), 0)
     q_half(slot(a2, b), 0, at(a, bp))
     got_half(slot(a2, b), 1)
@@ -258,6 +269,17 @@
     q_half(slot(a2, b), 1, at(a, bp))
     q_half(slot(a2, b), 0, at(a, bm))
     q_other(slot(a2, b))
+    got_half(slot(a, bm), 0)
+    q_half(slot(a, bm), 0, at(a, bp))
+    got_half(slot(a, bp), 1)
+    q_half(slot(a, bp), 1, at(a, bm))
+    pl.semaphore_wait(near_s.at[2], 2)
+
+    @pl.loop(0, 15)
+    def _(k):
+        zk = lax.rem(z + lax.rem(k + 5, 15) + 1, 16)
+        push(ab.at[kind, zcols], ab.at[kind, zcols], ab_s, ab_r, (dp, zk))
+
     arrive(pb.at[other_rows], p_r, p_s)
     (s_b,) = scores(b)
     for a_ in (am, ap):
@@ -265,9 +287,6 @@
         q_half(slot(a_, bm), 0, at(a, bp))
         got_half(slot(a_, bp), 1)
         q_half(slot(a_, bp), 1, at(a, bm))
-    counts_ready()
-    s_pos = jnp.sum(pos_hot * s_b, axis=0, keepdims=True)
-    statistics(b, s_b)
     got_half(slot(a2, bm), 0)
     q_half(slot(a2, bm), 0, at(a, bp))
     got_half(slot(a2, bp), 1)
@@ -278,6 +297,9 @@
         q_other(slot(a_, bm))
         q_other(slot(a_, bp))
     s_m, s_p = scores(bm, bp)
+    counts_ready()
+    s_pos = jnp.sum(pos_hot * s_b, axis=0, keepdims=True)
+    statistics(b, s_b)
     statistics(bm, s_m)
     statistics(bp, s_p)
     for a_ in (a, am, ap, a2):
@@ -290,7 +312,9 @@
     for a_ in (a, am, ap, a2):
         q_other(slot(a_, b2))
 
-    arrive(ab.at[:, 0 : 15 * 256], ab_r, ab_s)
+    arrive(ab.at[kind, 0 : 15 * 256], ab_r, ab_s)
+    ab_copy = push(ab.at[kind, :], ab.at[kind, :], abp_s, abp_r, partner)
+    arrive(ab.at[other_kind, :], abp_r, abp_s)
     loads[6].wait()
     loads[7].wait()
     low_rows = dot(aq_ref[...], ab[0:16, :], NT).astype(BF16).astype(F32) * q_inv
@@ -313,8 +337,8 @@
     top = srcv[0, :, 0:1, :]
     for s in range(1, 16):
         top = jnp.maximum(top, srcv[s, :, 0:1, :])
-    total = jnp.zeros((4, 1, 128), F32)
-    first = jnp.zeros((4, 1, 128), F32)
+    total = jnp.zeros((2, 1, 128), F32)
+    first = jnp.zeros((2, 1, 128), F32)
     for s in range(16):
         f = jnp.exp(srcv[s, :, 0:1, :] - top)
         total = total + f * srcv[s, :, 1:2, :]
@@ -322,20 +346,21 @@
     rows_s[:, 0:1, :] = jnp.exp(stat[:, 0:1, :] - top) * (HEAT / total)
     rows_s[:, 1:2, :] = first / total
     for i in range(4):
-        est[i] = est[i] * rows_s[i, 0:1, 0:64]
+        est[i] = est[i] * rows_s[i // 2, 0:1, i % 2 * 64 : i % 2 * 64 + 64]
     est[b] = est[b] - HEAT * pos_hot
     weight = jnp.concatenate([est[i] for i in range(4)], axis=1)
     w_hi, w_lo = hi_lo(weight)
     wt[0] = w_hi
     wt[1] = w_lo
     w_copy = push(wt.at[:, other_rows], woth, w_s, w_r, partner)
-    inner_row = rows_s[b, 1:2, 0:64] - s_pos
+    mean = rows_s[b // 2, 1:2, :]
+    inner_row = jnp.where(lax.rem(b, 2) == 0, mean[:, 0:64], mean[:, 64:128]) - s_pos
     inner = lanes_sum(jnp.where(own_lane, inner_row, 0.0))
 
+    share = dot(pbt, w_hi) + dot(pbt, w_lo)
+    share = share[0:16] + share[16:32]
     for i in range(4):
-        cols = slice(i * 64, (i + 1) * 64)
-        share = dot(pbt, w_hi[:, cols]) + dot(pbt, w_lo[:, cols])
-        ysnd[i, :, 0:64] = share[0:16] + share[16:32]
+        ysnd[i, :, 0:64] = share[:, i * 64 : (i + 1) * 64]
     peers(lambda a_, b_, s: push(ysnd.at[b_], yrcv.at[me], y_s, y_r, at(a_, b_)))
     yrcv[me] = ysnd[b]
     arrive(grcv.at[0:15], g_r, g_s)
@@ -372,6 +397,10 @@
     hop(0, t1.at[0], rl1.at[0], at(a, bp))
     shares(b2, 1, put_in(t1, 1))
     hop(1, t1.at[1], rl1.at[1], at(a, bm))
+    shares(bp, 1, put_in(d1p, 1))
+    hop(2, d1p.at[1], r1m.at[1], at(a, bp))
+    shares(bm, 0, put_in(d1m, 0))
+    hop(3, d1m.at[0], r1p.at[0], at(a, bm))
 
     def two_parts(w, q, h, sub):
         r = dot(w, q[:, h, :, sub].reshape(256, T))
@@ -423,8 +452,6 @@
     theirs = pl.ds(pl.multiple_of(other * 16, 16), 16)
     d_copy = push(dsum.at[theirs], dbuf, d_s, d_r, partner)
 
-    shares(bp, 1, put_in(d1p, 1))
-    shares(bm, 0, put_in(d1m, 0))
     shares(bp, 0, put_in(uf, 0))
     shares(bm, 1, put_in(uf, 1))
 
@@ -434,8 +461,6 @@
         drow[:, j // 2, j % 2, :] = dsum[mine, cols] + dbuf[:, cols]
     peers(lambda a_, b_, s: push(drow.at[s], rrow.at[me], rr_s, rr_r, at(a_, b_)))
     rrow[me] = drow[me]
-    hop(2, d1p.at[1], r1m.at[1], at(a, bp))
-    hop(3, d1m.at[0], r1p.at[0], at(a, bm))
     landed(rl1.at[0], 0)
     d1p[0] = (uf[0] + rl1[0].astype(F32)).astype(BF16)
     hop(4, d1p.at[0], r1m.at[0], at(a, bp))
@@ -503,11 +528,11 @@
     gq_out = pltpu.make_async_copy(gq_ref, gq_hbm, out_s.at[1])
     gq_out.start()
 
-    for c in rs + [p_copy, d_copy, w_copy]:
+    for c in rs + [p_copy, d_copy, w_copy, ab_copy]:
         c.wait_send()
     gone(qown.at[0:15], ag_s.at[0], q_r.at[0, 0])
     gone(qown, ag_s.at[1], qo_r)
-    gone(ab.at[:, 0 : 15 * 256], ab_s, ab_r)
+    gone(ab.at[kind, 0 : 15 * 256], ab_s, ab_r)
     gone(csnd.at[0:15], c_s, c_r)
     gone(srcv.at[0:15], s_s, s_r)
     gone(grcv.at[0:15], g_s, g_r)
@@ -577,9 +602,9 @@
             vm((16, 2, 16, 128), BF16),
             vm((4, 256, 64), F32),
             vm((4, 256, 64), F32),
-            vm((4, 4, 128), F32),
-            vm((16, 4, 4, 128), F32),
-            vm((4, 4, 128), F32),
+            vm((2, 4, 128), F32),
+            vm((16, 2, 4, 128), F32),
+            vm((2, 4, 128), F32),
             vm((2, 256, 256), BF16),
             vm((2, 128, 256), BF16),
             vm((2, 256, 256), BF16),
@@ -622,6 +647,9 @@
             dma(()),
             dma(()),
             dma(()),
+            pltpu.SemaphoreType.REGULAR((6,)),
+            dma(()),
+            dma(()),
             dma(()),
             dma(()),
             dma(()),

time: 69.6 us -> 67 us (0.963)
  Pallas kernels: 68.4 us -> 66.2 us
    pallas_call x1, Pallas kernels: 67.4 us -> 65.1 us  [per_device(): pl.pallas_call(kernel, out_shape=(jax.ShapeDtypeStruct((16, D), BF16), ja...]
where the time goes in v4:
time: 67 us; the launch traced here: 66.8 us
  Pallas kernels  66.2 us (99%)
    pallas_call x1, Pallas kernels, per_device(): pl.pallas_call(kernel, out_shape=(jax.ShapeDtypeStruct((16, D), BF16), ja...  65.1 us

profile of v4, /device:TPU:1, one launch (start us, length us, event | category | flops | bytes accessed | tf_op | source)
XLA Modules:
  0.0 66.8 jit_solution(9581674777503099100)
XLA Ops:
  0.6 65.1 %shard_map.120 = (bf16[16,4096]{1,0:T(8,128)(2,1)S(1)}, bf16[128,4096]{1,0:T(8,128)(2,1)S(1)}, f32[16,256]{1,0:T(8,128)S(1)}, f32[16,256]{1,0:T(8,128)S(1)}) custom-call(bf16[16,4096]{1,0:T(8,128)(2,1)} %bitcast.10, bf16[128,4096]{1,0:T(8,128)(2,1)} %bitcast.8, bf16[16,4096]{1,0:T(8,128)(2,1)} %bitcast.11, bf16[128,4096]{1,0:T(8,128)(2,1)} %bitcast.9, ...), custom_call_target="tpu_custom_call" | custom-call | tf_op jit(solution)/shard_map/pallas_call | solution.py:571
  65.8 1.0 %shard_map.121 = (bf16[16,4096]{1,0:T(8,128)(2,1)}, bf16[128,4096]{1,0:T(8,128)(2,1)}, f32[16,256]{1,0:T(8,128)}, f32[16,256]{1,0:T(8,128)}) custom-call(bf16[16,4096]{1,0:T(8,128)(2,1)S(1)} %get-tuple-element.12.refs_0_, bf16[128,4096]{1,0:T(8,128)(2,1)S(1)} %get-tuple-element.13.refs_1_, f32[16,256]{1,0:T(8,128)S(1)} %get-tuple-element.14.refs_2_, ...), custom_call_target="tpu_custom_call" | custom-call | tf_op jit(solution)/shard_map/pallas_call | solution.py:684

commit v5 on v4

--- a/solution.py
+++ b/solution.py
@@ -99,6 +99,48 @@
     qe = (qv * q_inv).astype(BF16)
     qown[me, 0] = qe[:, :H]
     qown[me, 1] = qe[:, H:]
+    pl.semaphore_wait(barrier, 7)
+    tell_z(near_s.at[0], 1)
+    tell_plane(near_s.at[3])
+
+    def push(src, dst, ssem, rsem, device):
+        c = pltpu.make_async_remote_copy(
+            src_ref=src, dst_ref=dst, send_sem=ssem, recv_sem=rsem, device_id=device, device_id_type=MESH
+        )
+        c.start()
+        return c
+
+    def arrive(dst, rsem, ssem):
+        pltpu.make_async_remote_copy(
+            src_ref=dst, dst_ref=dst, send_sem=ssem, recv_sem=rsem, device_id=partner, device_id_type=MESH
+        ).wait_recv()
+
+    def gone(src, ssem, rsem):
+        pltpu.make_async_remote_copy(
+            src_ref=src, dst_ref=src, send_sem=ssem, recv_sem=rsem, device_id=partner, device_id_type=MESH
+        ).wait_send()
+
+    def peers(body):
+        def one(k):
+            a_, b_ = near(a, lax.rem(6 - lax.rem(k, 4), 4)), near(b, lax.rem(6 - k // 4, 4))
+            body(a_, b_, slot(a_, b_))
+
+        pl.loop(0, 10)(one)
+        pl.loop(11, 16)(one)
+
+    def q_half(s, h, device):
+        push(qown.at[s, h], qown.at[s, h], ag_s.at[0], q_r.at[s, h], device)
+
+    def q_other(s):
+        push(qown.at[s], qoth.at[s], ag_s.at[1], qo_r, partner)
+
+    def got_half(s, h):
+        arrive(qown.at[s, h], q_r.at[s, h], ag_s.at[0])
+
+    q_half(me, 0, at(ap, b))
+    q_half(me, 1, at(am, b))
+    q_half(me, 1, at(ap, b))
+    q_half(me, 0, at(am, b))
     for i in (2, 3):
         loads[i].wait()
     zcols = pl.ds(pl.multiple_of(z * 256, 256), 256)
@@ -117,53 +159,15 @@
         return carry
 
     lax.fori_loop(0, 4, p_rows, 0)
-
-    pl.semaphore_wait(barrier, 7)
-    tell_z(near_s.at[0], 1)
-    tell_plane(near_s.at[3])
-
-    def push(src, dst, ssem, rsem, device):
-        c = pltpu.make_async_remote_copy(
-            src_ref=src, dst_ref=dst, send_sem=ssem, recv_sem=rsem, device_id=device, device_id_type=MESH
-        )
-        c.start()
-        return c
-
-    def arrive(dst, rsem, ssem):
-        pltpu.make_async_remote_copy(
-            src_ref=dst, dst_ref=dst, send_sem=ssem, recv_sem=rsem, device_id=partner, device_id_type=MESH
-        ).wait_recv()
-
-    def gone(src, ssem, rsem):
-        pltpu.make_async_remote_copy(
-            src_ref=src, dst_ref=src, send_sem=ssem, recv_sem=rsem, device_id=partner, device_id_type=MESH
-        ).wait_send()
-
-    def peers(body):
-        def one(k):
-            a_, b_ = near(a, lax.rem(6 - lax.rem(k, 4), 4)), near(b, lax.rem(6 - k // 4, 4))
-            body(a_, b_, slot(a_, b_))
-
-        pl.loop(0, 10)(one)
-        pl.loop(11, 16)(one)
-
-    def q_half(s, h, device):
-        push(qown.at[s, h], qown.at[s, h], ag_s.at[0], q_r.at[s, h], device)
-
-    def q_other(s):
-        push(qown.at[s], qoth.at[s], ag_s.at[1], qo_r, partner)
-
-    def got_half(s, h):
-        arrive(qown.at[s, h], q_r.at[s, h], ag_s.at[0])
-
-    q_half(me, 0, at(ap, b))
-    q_half(me, 1, at(am, b))
-    q_half(me, 1, at(ap, b))
-    q_half(me, 0, at(am, b))
     own_rows = pl.ds(pl.multiple_of(core * 128, 128), 128)
     other_rows = pl.ds(pl.multiple_of(other * 128, 128), 128)
     p_copy = push(pb.at[own_rows], pb.at[own_rows], p_s, p_r, partner)
     q_other(me)
+
+    q_half(me, 0, at(a, bp))
+    q_half(me, 1, at(a, bm))
+    q_half(me, 1, at(a, bp))
+    q_half(me, 0, at(a, bm))
 
     loads[4].wait()
     loads[5].wait()
@@ -176,11 +180,6 @@
         [(home >> 7).astype(F32).T, (home & 127).astype(F32).T], axis=0
     ).astype(BF16)
     for part in range(4):
-        if part == 1:
-            q_half(me, 0, at(a, bp))
-            q_half(me, 1, at(a, bm))
-            q_half(me, 1, at(a, bp))
-            q_half(me, 0, at(a, bm))
         n = n_row[:, part * T : (part + 1) * T]
         lane_q = (lax.broadcasted_iota(I32, (1, T), 1) >> 7) + part * 4
         picked = (lax.broadcasted_iota(I32, (32, T), 0) == (n >> 7)).astype(F32).astype(BF16)
@@ -363,11 +362,6 @@
         ysnd[i, :, 0:64] = share[:, i * 64 : (i + 1) * 64]
     peers(lambda a_, b_, s: push(ysnd.at[b_], yrcv.at[me], y_s, y_r, at(a_, b_)))
     yrcv[me] = ysnd[b]
-    arrive(grcv.at[0:15], g_r, g_s)
-    gall = grcv[...].reshape(256, 128)
-    xt = (dot(wt[0], gall) + dot(wt[1], gall)).T
-    xs = jnp.concatenate(hi_lo(xt[0:16] + xt[16:32]), axis=0)
-
     wq_hi, wq_lo = hi_lo(weight.T)
     wq[0] = wq_hi
     wq[1] = wq_lo
@@ -401,6 +395,11 @@
     hop(2, d1p.at[1], r1m.at[1], at(a, bp))
     shares(bm, 0, put_in(d1m, 0))
     hop(3, d1m.at[0], r1p.at[0], at(a, bm))
+
+    arrive(grcv.at[0:15], g_r, g_s)
+    gall = grcv[...].reshape(256, 128)
+    xt = (dot(wt[0], gall) + dot(wt[1], gall)).T
+    xs = jnp.concatenate(hi_lo(xt[0:16] + xt[16:32]), axis=0)
 
     def two_parts(w, q, h, sub):
         r = dot(w, q[:, h, :, sub].reshape(256, T))
@@ -497,6 +496,12 @@
             hop(8, t2.at[1], rl2.at[1], at(am, b))
             d2p[1] = v1[1, ap].astype(BF16)
             hop(9, d2p.at[1], r2m.at[1], at(ap, b))
+    landed(rl2.at[0], 6)
+    d2p[0] = (v1[0, ap] + rl2[0].astype(F32)).astype(BF16)
+    hop(10, d2p.at[0], r2m.at[0], at(ap, b))
+    landed(rl2.at[1], 8)
+    d2m[1] = (v1[1, am] + rl2[1].astype(F32)).astype(BF16)
+    hop(11, d2m.at[1], r2p.at[1], at(am, b))
     arrive(zbuf.at[0:15], z_r, z_s)
     acc = zbuf[0]
     for s in range(1, 16):
@@ -504,16 +509,14 @@
     orow[...] = acc
     oall[core * 16 + me] = acc
 
-    @pl.loop(1, 32)
-    def _(k):
-        push(orow, oall.at[core * 16 + me], o_s, o_r, (lax.rem(dp + k, 32), z))
-
-    landed(rl2.at[0], 6)
-    d2p[0] = (v1[0, ap] + rl2[0].astype(F32)).astype(BF16)
-    hop(10, d2p.at[0], r2m.at[0], at(ap, b))
-    landed(rl2.at[1], 8)
-    d2m[1] = (v1[1, am] + rl2[1].astype(F32)).astype(BF16)
-    hop(11, d2m.at[1], r2p.at[1], at(am, b))
+    def back_to_all(a_, b_, s):
+        row = core * 16 + me
+        push(orow, oall.at[row], o_s, o_r, at(a_, b_))
+        push(orow, oall.at[row], o_s, o_r, (a_ * sa + b_ * sb + other, z))
+
+    peers(back_to_all)
+    push(orow, oall.at[core * 16 + me], o_s, o_r, partner)
+
     landed(r2p.at[0], 7)
     landed(r2m.at[1], 9)
     landed(r2m.at[0], 10)

time: 67 us -> 65.6 us (0.979)
  Pallas kernels: 66.2 us -> 64.8 us
    pallas_call x1, Pallas kernels: 65.1 us -> 63.8 us  [per_device(): pl.pallas_call(kernel, out_shape=(jax.ShapeDtypeStruct((16, D), BF16), ja...]
where the time goes in v5:
time: 65.6 us; the launch traced here: 65.5 us
  Pallas kernels  64.8 us (99%)
    pallas_call x1, Pallas kernels, per_device(): pl.pallas_call(kernel, out_shape=(jax.ShapeDtypeStruct((16, D), BF16), ja...  63.8 us

profile of v5, /device:TPU:1, one launch (start us, length us, event | category | flops | bytes accessed | tf_op | source)
XLA Modules:
  0.0 65.5 jit_solution(13391952302640183330)
XLA Ops:
  0.6 63.8 %shard_map.120 = (bf16[16,4096]{1,0:T(8,128)(2,1)S(1)}, bf16[128,4096]{1,0:T(8,128)(2,1)S(1)}, f32[16,256]{1,0:T(8,128)S(1)}, f32[16,256]{1,0:T(8,128)S(1)}) custom-call(bf16[16,4096]{1,0:T(8,128)(2,1)} %bitcast.10, bf16[128,4096]{1,0:T(8,128)(2,1)} %bitcast.8, bf16[16,4096]{1,0:T(8,128)(2,1)} %bitcast.11, bf16[128,4096]{1,0:T(8,128)(2,1)} %bitcast.9, ...), custom_call_target="tpu_custom_call" | custom-call | tf_op jit(solution)/shard_map/pallas_call | solution.py:574
  64.4 1.0 %shard_map.121 = (bf16[16,4096]{1,0:T(8,128)(2,1)}, bf16[128,4096]{1,0:T(8,128)(2,1)}, f32[16,256]{1,0:T(8,128)}, f32[16,256]{1,0:T(8,128)}) custom-call(bf16[16,4096]{1,0:T(8,128)(2,1)S(1)} %get-tuple-element.12.refs_0_, bf16[128,4096]{1,0:T(8,128)(2,1)S(1)} %get-tuple-element.13.refs_1_, f32[16,256]{1,0:T(8,128)S(1)} %get-tuple-element.14.refs_2_, ...), custom_call_target="tpu_custom_call" | custom-call | tf_op jit(solution)/shard_map/pallas_call | solution.py:687

commit v6 on v5

--- a/solution.py
+++ b/solution.py
@@ -279,13 +279,13 @@
         zk = lax.rem(z + lax.rem(k + 5, 15) + 1, 16)
         push(ab.at[kind, zcols], ab.at[kind, zcols], ab_s, ab_r, (dp, zk))
 
-    arrive(pb.at[other_rows], p_r, p_s)
-    (s_b,) = scores(b)
     for a_ in (am, ap):
         got_half(slot(a_, bm), 0)
         q_half(slot(a_, bm), 0, at(a, bp))
         got_half(slot(a_, bp), 1)
         q_half(slot(a_, bp), 1, at(a, bm))
+    arrive(pb.at[other_rows], p_r, p_s)
+    (s_b,) = scores(b)
     got_half(slot(a2, bm), 0)
     q_half(slot(a2, bm), 0, at(a, bp))
     got_half(slot(a2, bp), 1)
@@ -391,10 +391,6 @@
     hop(0, t1.at[0], rl1.at[0], at(a, bp))
     shares(b2, 1, put_in(t1, 1))
     hop(1, t1.at[1], rl1.at[1], at(a, bm))
-    shares(bp, 1, put_in(d1p, 1))
-    hop(2, d1p.at[1], r1m.at[1], at(a, bp))
-    shares(bm, 0, put_in(d1m, 0))
-    hop(3, d1m.at[0], r1p.at[0], at(a, bm))
 
     arrive(grcv.at[0:15], g_r, g_s)
     gall = grcv[...].reshape(256, 128)
@@ -451,6 +447,8 @@
     theirs = pl.ds(pl.multiple_of(other * 16, 16), 16)
     d_copy = push(dsum.at[theirs], dbuf, d_s, d_r, partner)
 
+    shares(bp, 1, put_in(d1p, 1))
+    shares(bm, 0, put_in(d1m, 0))
     shares(bp, 0, put_in(uf, 0))
     shares(bm, 1, put_in(uf, 1))
 
@@ -460,6 +458,8 @@
         drow[:, j // 2, j % 2, :] = dsum[mine, cols] + dbuf[:, cols]
     peers(lambda a_, b_, s: push(drow.at[s], rrow.at[me], rr_s, rr_r, at(a_, b_)))
     rrow[me] = drow[me]
+    hop(2, d1p.at[1], r1m.at[1], at(a, bp))
+    hop(3, d1m.at[0], r1p.at[0], at(a, bm))
     landed(rl1.at[0], 0)
     d1p[0] = (uf[0] + rl1[0].astype(F32)).astype(BF16)
     hop(4, d1p.at[0], r1m.at[0], at(a, bp))
@@ -496,27 +496,27 @@
             hop(8, t2.at[1], rl2.at[1], at(am, b))
             d2p[1] = v1[1, ap].astype(BF16)
             hop(9, d2p.at[1], r2m.at[1], at(ap, b))
+    arrive(zbuf.at[0:15], z_r, z_s)
+    acc = zbuf[0]
+    for s in range(1, 16):
+        acc = acc + zbuf[s]
+    orow[...] = acc
+    oall[core * 16 + me] = acc
+
+    def back_to_all(a_, b_, s):
+        row = core * 16 + me
+        push(orow, oall.at[row], o_s, o_r, at(a_, b_))
+        push(orow, oall.at[row], o_s, o_r, (a_ * sa + b_ * sb + other, z))
+
+    peers(back_to_all)
+    push(orow, oall.at[core * 16 + me], o_s, o_r, partner)
+
     landed(rl2.at[0], 6)
     d2p[0] = (v1[0, ap] + rl2[0].astype(F32)).astype(BF16)
     hop(10, d2p.at[0], r2m.at[0], at(ap, b))
     landed(rl2.at[1], 8)
     d2m[1] = (v1[1, am] + rl2[1].astype(F32)).astype(BF16)
     hop(11, d2m.at[1], r2p.at[1], at(am, b))
-    arrive(zbuf.at[0:15], z_r, z_s)
-    acc = zbuf[0]
-    for s in range(1, 16):
-        acc = acc + zbuf[s]
-    orow[...] = acc
-    oall[core * 16 + me] = acc
-
-    def back_to_all(a_, b_, s):
-        row = core * 16 + me
-        push(orow, oall.at[row], o_s, o_r, at(a_, b_))
-        push(orow, oall.at[row], o_s, o_r, (a_ * sa + b_ * sb + other, z))
-
-    peers(back_to_all)
-    push(orow, oall.at[core * 16 + me], o_s, o_r, partner)
-
     landed(r2p.at[0], 7)
     landed(r2m.at[1], 9)
     landed(r2m.at[0], 10)

time: 65.6 us -> 66 us (level)
  no operation moved by 1% of the time
where the time goes in v6:
time: 66 us; the launch traced here: 65.9 us
  Pallas kernels  65.2 us (99%)
    pallas_call x1, Pallas kernels, per_device(): pl.pallas_call(kernel, out_shape=(jax.ShapeDtypeStruct((16, D), BF16), ja...  64.2 us

profile of v6, /device:TPU:1, one launch (start us, length us, event | category | flops | bytes accessed | tf_op | source)
XLA Modules:
  0.0 65.9 jit_solution(5474235018237544514)
XLA Ops:
  0.6 64.2 %shard_map.120 = (bf16[16,4096]{1,0:T(8,128)(2,1)S(1)}, bf16[128,4096]{1,0:T(8,128)(2,1)S(1)}, f32[16,256]{1,0:T(8,128)S(1)}, f32[16,256]{1,0:T(8,128)S(1)}) custom-call(bf16[16,4096]{1,0:T(8,128)(2,1)} %bitcast.10, bf16[128,4096]{1,0:T(8,128)(2,1)} %bitcast.8, bf16[16,4096]{1,0:T(8,128)(2,1)} %bitcast.11, bf16[128,4096]{1,0:T(8,128)(2,1)} %bitcast.9, ...), custom_call_target="tpu_custom_call" | custom-call | tf_op jit(solution)/shard_map/pallas_call | solution.py:574
  64.8 1.0 %shard_map.121 = (bf16[16,4096]{1,0:T(8,128)(2,1)}, bf16[128,4096]{1,0:T(8,128)(2,1)}, f32[16,256]{1,0:T(8,128)}, f32[16,256]{1,0:T(8,128)}) custom-call(bf16[16,4096]{1,0:T(8,128)(2,1)S(1)} %get-tuple-element.12.refs_0_, bf16[128,4096]{1,0:T(8,128)(2,1)S(1)} %get-tuple-element.13.refs_1_, f32[16,256]{1,0:T(8,128)S(1)} %get-tuple-element.14.refs_2_, ...), custom_call_target="tpu_custom_call" | custom-call | tf_op jit(solution)/shard_map/pallas_call | solution.py:687
